TPU v7x, 32 devices: a whole 2x2x4 slice. The times are simulated.
32 devices in a mesh: dp: 4 (over y, x), seq: 8 (over z, core).
Axes of the slice: x: 2, y: 2, z: 4, core: 2. Of those that a mesh axis runs over, the one named last changes fastest.
Arguments:
- tokens: bfloat16 [2, 16, 1024, 768], P(None, 'dp', 'seq'), may hold values from -6 to 6
- w_qkv: float32 [768, 2304], P(('dp', 'seq')), may hold values from -0.21875 to 0.21875
- w_feat: float32 [2, 768, 64], P(None, ('dp', 'seq')), may hold values from -1.5 to 1.5
- w_out: float32 [768, 768], P(('dp', 'seq')), may hold values from -0.875 to 0.875
- w_fc: float32 [768, 3072], P(('dp', 'seq')), may hold values from -0.21875 to 0.21875
- w_proj: float32 [3072, 768], P(('dp', 'seq')), may hold values from -0.109375 to 0.109375
- gains: float32 [2, 768], P(None, ('dp', 'seq')), may hold values from 0.5 to 1.5
- biases: float32 [11, 768], P(None, ('dp', 'seq')), may hold values from -0.6 to 0.6
- cotangent: bfloat16 [2, 16, 1024, 768], P(None, 'dp', 'seq'), may hold values from -6 to 6
Outputs:
- outputs: bfloat16 [2, 16, 1024, 768], P(None, 'dp', 'seq')
- input_grad: float32 [2, 16, 1024, 768], P(None, 'dp', 'seq')
- grad_qkv: float32 [768, 2304], P(('dp', 'seq'))
- grad_feat: float32 [2, 768, 64], P(None, ('dp', 'seq'))
- grad_out: float32 [768, 768], P(('dp', 'seq'))
- grad_fc: float32 [768, 3072], P(('dp', 'seq'))
- grad_proj: float32 [3072, 768], P(('dp', 'seq'))
- grad_gains: float32 [2, 768], P(None, ('dp', 'seq'))
- grad_biases: float32 [11, 768], P(None, ('dp', 'seq'))
All inputs are finite; a program needn't handle non-finite values.
Results may differ from a plain program's by a relative error of at most 0.017.
The roundings to bfloat16 on the way count: a program that leaves them out, or rounds other values in their place, can miss the bound.
Values may be sent and summed in bfloat16 or wider, within the bound.
No kernel may reach another device: no remote copies, remote signals or barrier semaphores. Data moves between devices by JAX's collectives and lax.ppermute only.
A program may use at most 320 MiB of HBM per device.

v0:
```python
import jax
import jax.numpy as jnp
from jax import lax
from jax.sharding import PartitionSpec as P

HD = 64
BLOCK = 64


def prefix(value, axis, combine, identity, reverse):
    devices, mine = (lax.axis_size(axis), lax.axis_index(axis))
    everything = jax.tree.map(
        lambda part, kind: lax.all_gather(part.astype(kind), axis),
        value,
        (jnp.bfloat16, jnp.bfloat16),
    )
    start = jax.tree.map(
        lambda part, zero: jnp.broadcast_to(jnp.asarray(zero, part.dtype), part.shape),
        value,
        identity,
    )

    def turn(k, before):
        at = devices - 1 - k if reverse else k
        reached = at > mine if reverse else at < mine
        new = combine(
            before, jax.tree.map(lambda part, own: part[at].astype(own.dtype), everything, value)
        )
        return jax.tree.map(lambda a, b: jnp.where(reached, a, b), new, before)

    return lax.fori_loop(0, devices, turn, start)


def layer_norm(values, norm_gain, norm_shift):
    centred = values - jnp.mean(values, axis=-1, keepdims=True)
    spread = jnp.mean(centred * centred, axis=-1, keepdims=True)
    return centred * lax.rsqrt(spread + 1e-05) * norm_gain + norm_shift


def features(logits):
    return jnp.concatenate(
        [jax.nn.softmax(logits, axis=-1), jax.nn.softmax(-logits, axis=-1)], axis=-1
    )


def gelu_tanh(values):
    return jax.nn.gelu(values, approximate=True)


def dot_plain(first_op, second_op):
    return jnp.dot(first_op, second_op, preferred_element_type=jnp.float32)


def dot_first(first_op, second_op):
    return lax.dot_general(
        first_op, second_op, (((0,), (0,)), ((), ())), preferred_element_type=jnp.float32
    )


def dot_second(first_op, second_op):
    return lax.dot_general(
        first_op, second_op, (((1,), (1,)), ((), ())), preferred_element_type=jnp.float32
    )


def add_pairs(earlier, later):
    return (earlier[0] + later[0], earlier[1] + later[1])


def earlier_sum(values):
    zero_row = jnp.zeros_like(values[:, :1])
    return jnp.concatenate([zero_row, jnp.cumsum(values[:, :-1], axis=1)], axis=1)


def later_sum(values):
    return jnp.flip(earlier_sum(jnp.flip(values, 1)), 1)


def forward_pass(gathered, inputs, seq_count, seg_len):
    w_qkv, w_feat, w_out, w_fc, w_proj, gains, biases = gathered
    gains_f = gains.astype(jnp.float32)
    biases_f = biases.astype(jnp.float32)
    tok_rows, model_width = inputs.shape
    head_count = model_width // HD
    block_count = seg_len // BLOCK
    blocked = (seq_count, block_count, BLOCK, head_count)
    hidden = layer_norm(inputs, gains_f[0], biases_f[0]).astype(jnp.bfloat16)
    mixed = (dot_plain(hidden, w_qkv) + biases_f[1:4].reshape(-1)).astype(jnp.bfloat16)
    queries = mixed[:, :model_width].reshape(tok_rows, head_count, HD)
    key_rows = mixed[:, model_width : 2 * model_width].reshape(tok_rows, head_count, HD)
    value_rows = mixed[:, 2 * model_width :].reshape(blocked + (HD,))
    logit_q = jnp.einsum(
        "rhi,hij->rhj",
        queries,
        w_feat[0].reshape(head_count, HD, HD),
        preferred_element_type=jnp.float32,
    )
    logit_k = jnp.einsum(
        "rhi,hij->rhj",
        key_rows,
        w_feat[1].reshape(head_count, HD, HD),
        preferred_element_type=jnp.float32,
    )
    phi_q = features(logit_q).astype(jnp.bfloat16).reshape(blocked + (2 * HD,))
    phi_k = features(logit_k).astype(jnp.bfloat16).reshape(blocked + (2 * HD,))
    causal = jnp.tril(jnp.ones((BLOCK, BLOCK), jnp.float32))
    scores = (
        jnp.einsum("snthf,snuhf->snhtu", phi_q, phi_k, preferred_element_type=jnp.float32) * causal
    ).astype(jnp.bfloat16)
    numerator = jnp.einsum(
        "snhtu,snuhe->snthe", scores, value_rows, preferred_element_type=jnp.float32
    )
    denominator = jnp.swapaxes(jnp.sum(scores, axis=-1, dtype=jnp.float32), 2, 3)
    own_state = jnp.einsum(
        "snuhf,snuhe->snhfe", phi_k, value_rows, preferred_element_type=jnp.float32
    )
    own_sum = jnp.sum(phi_k, axis=2, dtype=jnp.float32)
    dev_state = jnp.sum(own_state, axis=1)
    dev_sum = jnp.sum(own_sum, axis=1)
    before_state, before_sum = prefix(
        (dev_state, dev_sum),
        "seq",
        add_pairs,
        (jnp.zeros_like(dev_state), jnp.zeros_like(dev_sum)),
        False,
    )
    prior_state = (before_state[:, None] + earlier_sum(own_state)).astype(jnp.bfloat16)
    prior_sum = before_sum[:, None] + earlier_sum(own_sum)
    numerator = numerator + jnp.einsum(
        "snthf,snhfe->snthe", phi_q, prior_state, preferred_element_type=jnp.float32
    )
    denominator = denominator + jnp.einsum(
        "snthf,snhf->snth", phi_q, prior_sum, preferred_element_type=jnp.float32
    )
    contexts = numerator / denominator[..., None]
    merged = contexts.reshape(tok_rows, model_width).astype(jnp.bfloat16)
    middle = inputs + dot_plain(merged, w_out) + biases_f[4]
    normed = layer_norm(middle, gains_f[1], biases_f[5]).astype(jnp.bfloat16)
    pre_act = dot_plain(normed, w_fc) + biases_f[6:10].reshape(-1)
    activated = gelu_tanh(pre_act).astype(jnp.bfloat16)
    result = middle + dot_plain(activated, w_proj) + biases_f[10]
    saved = (
        inputs,
        hidden,
        queries,
        key_rows,
        value_rows,
        logit_q,
        logit_k,
        phi_q,
        phi_k,
        prior_state,
        prior_sum,
        contexts,
        denominator,
        merged,
        middle,
        normed,
        pre_act,
        activated,
    )
    return (result, saved)


def backward_pass(gathered, saved, upstream):
    w_qkv, w_feat, w_out, w_fc, w_proj, gains, biases = gathered
    (
        inputs,
        hidden,
        queries,
        key_rows,
        value_rows,
        logit_q,
        logit_k,
        phi_q,
        phi_k,
        prior_state,
        prior_sum,
        contexts,
        denominator,
        merged,
        middle,
        normed,
        pre_act,
        activated,
    ) = saved
    gains_f = gains.astype(jnp.float32)
    biases_f = biases.astype(jnp.float32)
    tok_rows, model_width = inputs.shape
    head_count = model_width // HD
    d_mlp = upstream.astype(jnp.bfloat16)
    grad_proj = dot_first(activated, d_mlp)
    bias_proj = jnp.sum(d_mlp, axis=0, dtype=jnp.float32)
    d_act = dot_second(d_mlp, w_proj)
    gelu_back = jax.vjp(gelu_tanh, pre_act)[1]
    d_pre = gelu_back(d_act)[0].astype(jnp.bfloat16)
    grad_fc = dot_first(normed, d_pre)
    bias_fc = jnp.sum(d_pre, axis=0, dtype=jnp.float32)
    d_normed = dot_second(d_pre, w_fc)
    norm_back_two = jax.vjp(layer_norm, middle, gains_f[1], biases_f[5])[1]
    d_middle, gain_two, shift_two = norm_back_two(d_normed)
    d_middle = d_middle + upstream
    d_branch = d_middle.astype(jnp.bfloat16)
    grad_out = dot_first(merged, d_branch)
    bias_out = jnp.sum(d_branch, axis=0, dtype=jnp.float32)
    d_context = dot_second(d_branch, w_out).reshape(contexts.shape)
    d_numer = (d_context / denominator[..., None]).astype(jnp.bfloat16)
    d_denom = -jnp.sum(d_context * contexts, axis=-1) / denominator
    causal = jnp.tril(jnp.ones((BLOCK, BLOCK), jnp.float32))
    scores = (
        jnp.einsum("snthf,snuhf->snhtu", phi_q, phi_k, preferred_element_type=jnp.float32) * causal
    ).astype(jnp.bfloat16)
    d_scores = jnp.einsum(
        "snthe,snuhe->snhtu", d_numer, value_rows, preferred_element_type=jnp.float32
    )
    d_scores = ((d_scores + jnp.swapaxes(d_denom, 2, 3)[..., None]) * causal).astype(jnp.bfloat16)
    d_values = jnp.einsum("snhtu,snthe->snuhe", scores, d_numer, preferred_element_type=jnp.float32)
    d_phi_q = jnp.einsum("snhtu,snuhf->snthf", d_scores, phi_k, preferred_element_type=jnp.float32)
    d_phi_q = d_phi_q + jnp.einsum(
        "snthe,snhfe->snthf", d_numer, prior_state, preferred_element_type=jnp.float32
    )
    d_phi_q = d_phi_q + d_denom[..., None] * prior_sum[:, :, None]
    d_phi_k = jnp.einsum("snhtu,snthf->snuhf", d_scores, phi_q, preferred_element_type=jnp.float32)
    d_state = jnp.einsum("snthf,snthe->snhfe", phi_q, d_numer, preferred_element_type=jnp.float32)
    d_sum = jnp.einsum("snthf,snth->snhf", phi_q, d_denom, preferred_element_type=jnp.float32)
    dev_state = jnp.sum(d_state, axis=1)
    dev_sum = jnp.sum(d_sum, axis=1)
    after_state, after_sum = prefix(
        (dev_state, dev_sum),
        "seq",
        add_pairs,
        (jnp.zeros_like(dev_state), jnp.zeros_like(dev_sum)),
        True,
    )
    d_own = (after_state[:, None] + later_sum(d_state)).astype(jnp.bfloat16)
    d_own_sum = after_sum[:, None] + later_sum(d_sum)
    d_phi_k = d_phi_k + jnp.einsum(
        "snuhe,snhfe->snuhf", value_rows, d_own, preferred_element_type=jnp.float32
    )
    d_phi_k = d_phi_k + d_own_sum[:, :, None]
    d_values = d_values + jnp.einsum(
        "snuhf,snhfe->snuhe", phi_k, d_own, preferred_element_type=jnp.float32
    )
    feat_back_q = jax.vjp(features, logit_q)[1]
    feat_back_k = jax.vjp(features, logit_k)[1]
    d_logit_q = feat_back_q(d_phi_q.reshape(tok_rows, head_count, 2 * HD))[0].astype(jnp.bfloat16)
    d_logit_k = feat_back_k(d_phi_k.reshape(tok_rows, head_count, 2 * HD))[0].astype(jnp.bfloat16)
    map_q = w_feat[0].reshape(head_count, HD, HD)
    map_k = w_feat[1].reshape(head_count, HD, HD)
    d_queries = jnp.einsum("rhj,hij->rhi", d_logit_q, map_q, preferred_element_type=jnp.float32)
    d_keys = jnp.einsum("rhj,hij->rhi", d_logit_k, map_k, preferred_element_type=jnp.float32)
    grad_map_q = jnp.einsum("rhi,rhj->hij", queries, d_logit_q, preferred_element_type=jnp.float32)
    grad_map_k = jnp.einsum("rhi,rhj->hij", key_rows, d_logit_k, preferred_element_type=jnp.float32)
    d_qkv = jnp.concatenate(
        [
            d_queries.reshape(tok_rows, model_width),
            d_keys.reshape(tok_rows, model_width),
            d_values.reshape(tok_rows, model_width),
        ],
        axis=1,
    ).astype(jnp.bfloat16)
    grad_qkv = dot_first(hidden, d_qkv)
    bias_qkv = jnp.sum(d_qkv, axis=0, dtype=jnp.float32)
    d_hidden = dot_second(d_qkv, w_qkv)
    norm_back_one = jax.vjp(layer_norm, inputs, gains_f[0], biases_f[0])[1]
    d_input, gain_one, shift_one = norm_back_one(d_hidden)
    input_grad = d_input + d_middle
    grad_feat = jnp.stack(
        [grad_map_q.reshape(model_width, HD), grad_map_k.reshape(model_width, HD)]
    )
    grad_gains = jnp.stack([gain_one, gain_two])
    grad_biases = jnp.concatenate(
        [
            shift_one[None],
            bias_qkv.reshape(3, model_width),
            bias_out[None],
            shift_two[None],
            bias_fc.reshape(4, model_width),
            bias_proj[None],
        ],
        axis=0,
    )
    grads = (grad_qkv, grad_feat, grad_out, grad_fc, grad_proj, grad_gains, grad_biases)
    return (grads, input_grad)


def shards(tokens, w_qkv, w_feat, w_out, w_fc, w_proj, gains, biases, cotangent):
    micro_count, seq_count, seg_len, model_width = tokens.shape
    hidden_width = w_fc.shape[1]
    masters = (w_qkv, w_feat, w_out, w_fc, w_proj, gains, biases)
    copies = tuple((master.astype(jnp.bfloat16) for master in masters))
    summed = (
        jnp.zeros((model_width, 3 * model_width), jnp.float32),
        jnp.zeros((2, model_width, HD), jnp.float32),
        jnp.zeros((model_width, model_width), jnp.float32),
        jnp.zeros((model_width, hidden_width), jnp.float32),
        jnp.zeros((hidden_width, model_width), jnp.float32),
        jnp.zeros((2, model_width), jnp.float32),
        jnp.zeros((11, model_width), jnp.float32),
    )
    results = []
    input_grads = []
    for micro_index in range(micro_count):
        gathered = (
            lax.all_gather(copies[0], ("dp", "seq"), axis=0, tiled=True),
            lax.all_gather(copies[1], ("dp", "seq"), axis=1, tiled=True),
            lax.all_gather(copies[2], ("dp", "seq"), axis=0, tiled=True),
            lax.all_gather(copies[3], ("dp", "seq"), axis=0, tiled=True),
            lax.all_gather(copies[4], ("dp", "seq"), axis=0, tiled=True),
            lax.all_gather(copies[5], ("dp", "seq"), axis=1, tiled=True),
            lax.all_gather(copies[6], ("dp", "seq"), axis=1, tiled=True),
        )
        inputs = tokens[micro_index].reshape(-1, model_width).astype(jnp.float32)
        result, saved = forward_pass(gathered, inputs, seq_count, seg_len)
        results.append(result.reshape(seq_count, seg_len, model_width).astype(jnp.bfloat16))
        again = (
            lax.all_gather(copies[0], ("dp", "seq"), axis=0, tiled=True),
            lax.all_gather(copies[1], ("dp", "seq"), axis=1, tiled=True),
            lax.all_gather(copies[2], ("dp", "seq"), axis=0, tiled=True),
            lax.all_gather(copies[3], ("dp", "seq"), axis=0, tiled=True),
            lax.all_gather(copies[4], ("dp", "seq"), axis=0, tiled=True),
            lax.all_gather(copies[5], ("dp", "seq"), axis=1, tiled=True),
            lax.all_gather(copies[6], ("dp", "seq"), axis=1, tiled=True),
        )
        upstream = cotangent[micro_index].reshape(-1, model_width).astype(jnp.float32)
        grads, input_grad = backward_pass(again, saved, upstream)
        input_grads.append(input_grad.reshape(seq_count, seg_len, model_width))
        summed = tuple((held + fresh for held, fresh in zip(summed, grads)))
    finals = (
        lax.psum_scatter(summed[0], ("dp", "seq"), scatter_dimension=0, tiled=True),
        lax.psum_scatter(summed[1], ("dp", "seq"), scatter_dimension=1, tiled=True),
        lax.psum_scatter(summed[2], ("dp", "seq"), scatter_dimension=0, tiled=True),
        lax.psum_scatter(summed[3], ("dp", "seq"), scatter_dimension=0, tiled=True),
        lax.psum_scatter(summed[4], ("dp", "seq"), scatter_dimension=0, tiled=True),
        lax.psum_scatter(summed[5], ("dp", "seq"), scatter_dimension=1, tiled=True),
        lax.psum_scatter(summed[6], ("dp", "seq"), scatter_dimension=1, tiled=True),
    )
    return (
        jnp.stack(results),
        jnp.stack(input_grads),
        finals[0],
        finals[1],
        finals[2],
        finals[3],
        finals[4],
        finals[5],
        finals[6],
    )


def solution(mesh):
    return jax.shard_map(
        shards,
        mesh=mesh,
        in_specs=(
            P(None, "dp", "seq", None),
            P(("dp", "seq"), None),
            P(None, ("dp", "seq"), None),
            P(("dp", "seq"), None),
            P(("dp", "seq"), None),
            P(("dp", "seq"), None),
            P(None, ("dp", "seq")),
            P(None, ("dp", "seq")),
            P(None, "dp", "seq", None),
        ),
        out_specs=(
            P(None, "dp", "seq", None),
            P(None, "dp", "seq", None),
            P(("dp", "seq"), None),
            P(None, ("dp", "seq"), None),
            P(("dp", "seq"), None),
            P(("dp", "seq"), None),
            P(("dp", "seq"), None),
            P(None, ("dp", "seq")),
            P(None, ("dp", "seq")),
        ),
        check_vma=False,
    )
```

profile of v0, /device:TPU:0, one launch (start us, length us, event | category | flops | bytes accessed | tf_op | source)
XLA Modules:
  0.0 1354.9 jit_solution(143630189826766961)
XLA Ops:
  11.4 43.9 %all-gather.9 = bf16[32,24,11]{1,2,0:T(8,128)(2,1)S(1)} all-gather(bf16[1,24,11]{1,2,0:T(8,128)(2,1)S(1)} %convert_bitcast_fusion), channel_id=1, replica_groups=mesh['dp'=4,'seq'=8] {'dp','seq'}, dimensions={0}, use_global_device_ids=true | all-gather | bytes 17424 | tf_op jit(solution)/shard_map/all_gather | solution.py:311
  55.8 36.6 %all-gather.8 = bf16[32,24,2]{1,2,0:T(2,128)(2,1)S(1)} all-gather(bf16[1,24,2]{1,2,0:T(2,128)(2,1)S(1)} %convert_bitcast_fusion.1), channel_id=1, replica_groups=mesh['dp'=4,'seq'=8] {'dp','seq'}, dimensions={0}, use_global_device_ids=true | all-gather | bytes 3168 | tf_op jit(solution)/shard_map/all_gather | solution.py:310
  92.7 40.7 %all_gather.37 = bf16[2,768,64]{2,1,0:T(8,128)(2,1)S(1)} all-gather(bf16[2,24,64]{2,1,0:T(8,128)(2,1)S(1)} %convert_element_type.407), channel_id=1, replica_groups=mesh['dp'=4,'seq'=8] {'dp','seq'}, dimensions={1}, use_global_device_ids=true | all-gather | bytes 202752 | tf_op jit(solution)/shard_map/all_gather | solution.py:306
  257.2 15.7 %all-gather.1 = bf16[32,12,128]{2,1,0:T(8,128)(2,1)} all-gather(bf16[4,12,128]{2,1,0:T(8,128)(2,1)} %get-tuple-element.769), channel_id=3, replica_groups=mesh['dp'=4,'seq'=8] {'seq'}, dimensions={0}, use_global_device_ids=true | all-gather | bytes 110592 | tf_op jit(solution)/shard_map/all_gather | solution.py:13
  305.9 15.1 %all-gather.3 = bf16[32,12,128]{2,1,0:T(8,128)(2,1)} all-gather(bf16[4,12,128]{2,1,0:T(8,128)(2,1)S(1)} %copy-done.175), channel_id=5, replica_groups=mesh['dp'=4,'seq'=8] {'seq'}, dimensions={0}, use_global_device_ids=true | all-gather | bytes 110592 | tf_op jit(solution)/shard_map/all_gather | solution.py:13
  345.3 6.9 fusion.180
  352.2 54.1 %while.68 = (s32[]{:T(128)}, f32[4,12,128,64]{3,2,1,0:T(8,128)}, f32[4,12,128]{2,1,0:T(8,128)S(1)}, s32[]{:T(128)}, bf16[8,4,12,128,64]{3,4,2,1,0:T(8,128)(2,1)}...) while((s32[]{:T(128)}, f32[4,12,128,64]{3,2,1,0:T(8,128)}, ...), condition=%wide.region_13.14_spmd.clone, body=%wide.region_12.13_spmd.clone.sunk | while | flops 1597444 | bytes 7139443 | solution.py:31
  418.8 54.4 %while.69 = (s32[]{:T(128)}, f32[4,12,128,64]{3,2,1,0:T(8,128)}, f32[4,12,128]{2,1,0:T(8,128)S(1)}, s32[]{:T(128)}, bf16[8,4,12,128,64]{3,4,2,1,0:T(8,128)(2,1)}...) while((s32[]{:T(128)}, f32[4,12,128,64]{3,2,1,0:T(8,128)}, ...), condition=%wide.region_31.32_spmd.clone, body=%wide.region_30.31_spmd.clone.sunk | while | flops 1597444 | bytes 7139443 | solution.py:31
  491.7 8.4 fusion.141
  505.0 15.6 %convert_reduce_fusion.1 = (f32[3072]{0:T(1024)}, bf16[512,3072]{1,0:T(8,128)(2,1)}, f32[3072]{0:T(1024)}, bf16[512,3072]{1,0:T(8,128)(2,1)S(1)}) fusion(f32[512,3072]{1,0:T(8,128)} %fusion.141, f32[3072]{0:T(1024)S(1)} %copy-done.199, f32[512,3072]{1,0:T(8,128)} %fusion.180, f32[512,3072]{1,0:T(8,128)} %fusion.142, bf16[512,768]{1,0:T(8,128)(2,1)S(1)} %bitcast.458, ...), kind=kOutput, calls=%fused_computation.39 | convolution fusion | flops 2488264704 | bytes 30707712 | tf_op jit(solution)/shard_map/dot_general | solution.py:61
  626.9 15.4 %all-gather.7 = bf16[32,12,128]{2,1,0:T(8,128)(2,1)} all-gather(bf16[4,12,128]{2,1,0:T(8,128)(2,1)S(1)} %fusion.124), channel_id=9, replica_groups=mesh['dp'=4,'seq'=8] {'seq'}, dimensions={0}, use_global_device_ids=true | all-gather | bytes 110592 | tf_op jit(solution)/shard_map/all_gather | solution.py:13
  642.4 15.8 %all-gather.5 = bf16[32,12,128]{2,1,0:T(8,128)(2,1)} all-gather(bf16[4,12,128]{2,1,0:T(8,128)(2,1)S(1)} %fusion.123), channel_id=7, replica_groups=mesh['dp'=4,'seq'=8] {'seq'}, dimensions={0}, use_global_device_ids=true | all-gather | bytes 110592 | tf_op jit(solution)/shard_map/all_gather | solution.py:13
  672.9 7.2 fusion.140
  680.8 54.8 %while.71 = (s32[]{:T(128)}, f32[4,12,128,64]{3,2,1,0:T(8,128)}, f32[4,12,128]{2,1,0:T(8,128)S(1)}, s32[]{:T(128)}, bf16[8,4,12,128,64]{3,4,2,1,0:T(8,128)(2,1)}...) while((s32[]{:T(128)}, f32[4,12,128,64]{3,2,1,0:T(8,128)}, ...), condition=%wide.region_57.58_spmd.clone, body=%wide.region_56.57_spmd.clone.sunk | while | flops 1597448 | bytes 7139505 | solution.py:31
  757.6 59.6 %while.70 = (s32[]{:T(128)}, f32[4,12,128,64]{3,2,1,0:T(8,128)}, f32[4,12,128]{2,1,0:T(8,128)}, s32[]{:T(128)}, bf16[8,4,12,128,64]{3,4,2,1,0:T(8,128)(2,1)}, /*...) while((s32[]{:T(128)}, f32[4,12,128,64]{3,2,1,0:T(8,128)}, ...), condition=%wide.region_44.45_spmd.clone, body=%wide.region_43.44_spmd.clone.sunk | while | flops 1597448 | bytes 7336169 | solution.py:31
  847.6 8.6 convolution_add_fusion.2
  857.4 5.9 fusion.143
  863.3 10.1 convolution_add_fusion.1
  914.9 8.6 add_convert_fusion.12
  923.5 8.3 add_convert_fusion.10
  946.8 38.3 %all-reduce.10 = (f32[2,768]{1,0:T(2,128)S(1)}, f32[11,768]{1,0:T(8,128)S(1)}) all-reduce(f32[2,768]{1,0:T(2,128)S(1)} %maximum_add_fusion.1, f32[11,768]{1,0:T(8,128)S(1)} %add.681), channel_id=15, replica_groups=mesh['dp'=4,'seq'=8] {'dp','seq'}, use_global_device_ids=true, to_apply=%region_71.72.clone | all-reduce | flops 9984 | bytes 79872
  992.2 89.8 %reduce-scatter.14.cloned.1.call-done = f32[24,3072]{1,0:T(8,128)} async-done(((f32[768,3072]{1,0:T(8,128)}), f32[24,3072]{1,0:T(8,128)}) %reduce-scatter.14.cloned.1.call-update) | async-done | bytes 294928 | tf_op jit(solution)/shard_map/reduce_scatter | solution.py:333
  1081.9 141.0 %reduce-scatter.16.cloned.1.call-done = f32[96,768]{1,0:T(8,128)} async-done(((f32[3072,768]{1,0:T(8,128)}), f32[96,768]{1,0:T(8,128)}) %reduce-scatter.16.cloned.1.call-update) | async-done | bytes 294928 | tf_op jit(solution)/shard_map/reduce_scatter | solution.py:334
  1223.0 125.2 %reduce-scatter.8.cloned.1.call-done = f32[24,2304]{1,0:T(8,128)} async-done(((f32[768,2304]{1,0:T(8,128)}), f32[24,2304]{1,0:T(8,128)}) %reduce-scatter.8.cloned.1.call-update) | async-done | bytes 221200 | tf_op jit(solution)/shard_map/reduce_scatter | solution.py:330
  (904 shorter events, 680.3 us)
Async XLA Ops:
  7.2 85.5 %copy-start.186 = (f32[2,24,64]{2,1,0:T(8,128)S(1)}, f32[2,24,64]{2,1,0:T(8,128)}, u32[]{:S(2)}) copy-start(f32[2,24,64]{2,1,0:T(8,128)} %param.19) | copy-start | bytes 36868
  7.2 126.9 %copy-start = (bf16[2,4,128,768]{3,2,1,0:T(8,128)(2,1)S(1)}, bf16[2,4,128,768]{3,2,1,0:T(8,128)(2,1)}, u32[]{:S(2)}) copy-start(bf16[2,4,128,768]{3,2,1,0:T(8,128)(2,1)} %param.17) | copy-start | bytes 4718596
  7.2 129.9 %all-gather.19.cloned.1.call-start = ((), (), s32[]{:S(2)}) async-start(), calls=%async_computation.5 | async-start | bytes 3649536 | tf_op jit(solution)/shard_map/all_gather | solution.py:305
  9.0 336.1 %all-gather.25.cloned.1.call-start = ((), (), s32[]{:S(2)}) async-start(), calls=%async_computation.8 | async-start | bytes 4866048 | tf_op jit(solution)/shard_map/all_gather | solution.py:309
  10.7 341.5 %all-gather.27.cloned.1.call-start = ((), (), s32[]{:S(2)}) async-start(), calls=%async_computation.14 | async-start | bytes 7077888 | tf_op jit(solution)/shard_map/all_gather | solution.py:13
  55.8 79.2 %copy-start.163 = (f32[768,11]{0,1:T(8,128)}, f32[768,11]{0,1:T(8,128)S(1)}, u32[]{:S(2)}) copy-start(f32[768,11]{0,1:T(8,128)S(1)} %reshape.561) | copy-start | bytes 101380
  135.1 70.7 %copy-start.75 = (bf16[1,768,64]{2,1,0:T(8,128)(2,1)}, bf16[1,768,64]{2,1,0:T(8,128)(2,1)S(1)}, u32[]{:S(2)}) copy-start(bf16[1,768,64]{2,1,0:T(8,128)(2,1)S(1)} %get-tuple-element.799) | copy-start | bytes 294916
  135.1 119.1 %copy-start.77 = (bf16[1,768,64]{2,1,0:T(8,128)(2,1)}, bf16[1,768,64]{2,1,0:T(8,128)(2,1)S(1)}, u32[]{:S(2)}) copy-start(bf16[1,768,64]{2,1,0:T(8,128)(2,1)S(1)} %get-tuple-element.800) | copy-start | bytes 294916
  178.9 121.0 %copy-start.2 = (bf16[4,2,64,12,128]{4,2,3,1,0:T(8,128)(2,1)}, bf16[4,2,64,12,128]{4,2,3,1,0:T(8,128)(2,1)S(1)}, u32[]{:S(2)}) copy-start(bf16[4,2,64,12,128]{4,2,3,1,0:T(8,128)(2,1)S(1)} %get-tuple-element.770) | copy-start | bytes 4718596
  182.4 236.4 %all-gather.29.cloned.1.call-start = ((), (), s32[]{:S(2)}) async-start(), calls=%async_computation.15 | async-start | bytes 7077888 | tf_op jit(solution)/shard_map/all_gather | solution.py:13
  232.1 253.6 %all-gather.21.cloned.1.call-start = ((), (), s32[]{:S(2)}) async-start(), calls=%async_computation.6 | async-start | bytes 1216512 | tf_op jit(solution)/shard_map/all_gather | solution.py:307
  232.8 258.9 %all-gather.23.cloned.1.call-start = ((), (), s32[]{:S(2)}) async-start(), calls=%async_computation.7 | async-start | bytes 4866048 | tf_op jit(solution)/shard_map/all_gather | solution.py:308
  234.5 446.0 %all-gather.33.cloned.1.call-start = ((), (), s32[]{:S(2)}) async-start(), calls=%async_computation.17 | async-start | bytes 7077888 | tf_op jit(solution)/shard_map/all_gather | solution.py:13
  254.2 66.8 %copy-start.143 = (f32[512,12]{0,1:T(8,128)}, f32[512,12]{0,1:T(8,128)S(1)}, u32[]{:S(2)}) copy-start(f32[512,12]{0,1:T(8,128)S(1)} %get-tuple-element.814) | copy-start | bytes 73732
  257.2 71.2 %copy-start.147 = (f32[512,12]{0,1:T(8,128)}, f32[512,12]{0,1:T(8,128)S(1)}, u32[]{:S(2)}) copy-start(f32[512,12]{0,1:T(8,128)S(1)} %get-tuple-element.812) | copy-start | bytes 73732
  273.7 135.1 %copy-start.153 = (f32[4,1,12,128]{3,2,1,0:T(8,128)}, f32[4,1,12,128]{3,2,1,0:T(8,128)S(1)}, u32[]{:S(2)}) copy-start(f32[4,1,12,128]{3,2,1,0:T(8,128)S(1)} %slice.143) | copy-start | bytes 73732
  321.0 154.9 %copy-start.155 = (f32[4,1,12,128]{3,2,1,0:T(8,128)}, f32[4,1,12,128]{3,2,1,0:T(8,128)S(1)}, u32[]{:S(2)}) copy-start(f32[4,1,12,128]{3,2,1,0:T(8,128)S(1)} %slice.153) | copy-start | bytes 73732
  340.3 136.5 %copy-start.136 = (f32[4,2,12,64]{3,2,1,0:T(8,128)}, f32[4,2,12,64]{3,2,1,0:T(8,128)S(1)}, u32[]{:S(2)}) copy-start(f32[4,2,12,64]{3,2,1,0:T(8,128)S(1)} %get-tuple-element.820) | copy-start | bytes 73732
  544.5 213.1 %all-gather.31.cloned.1.call-start = ((), (), s32[]{:S(2)}) async-start(), calls=%async_computation.16 | async-start | bytes 7077888 | tf_op jit(solution)/shard_map/all_gather | solution.py:13
  564.3 427.8 %reduce-scatter.12.cloned.1.call-start = ((), (), s32[]{:S(2)}) async-start(), calls=%async_computation.11 | async-start | bytes 2433024 | tf_op jit(solution)/shard_map/reduce_scatter | solution.py:332
  680.1 312.1 %reduce-scatter.10.cloned.1.call-start = ((), (), s32[]{:S(2)}) async-start(), calls=%async_computation.10 | async-start | bytes 811008 | tf_op jit(solution)/shard_map/reduce_scatter | solution.py:331
  846.9 235.0 %reduce-scatter.14.cloned.1.call-start = ((), (), s32[]{:S(2)}) async-start(), calls=%async_computation.12 | async-start | bytes 9732096 | tf_op jit(solution)/shard_map/reduce_scatter | solution.py:333
  856.3 366.7 %reduce-scatter.16.cloned.1.call-start = ((), (), s32[]{:S(2)}) async-start(), calls=%async_computation.13 | async-start | bytes 9732096 | tf_op jit(solution)/shard_map/reduce_scatter | solution.py:334
  873.5 474.7 %reduce-scatter.8.cloned.1.call-start = ((), (), s32[]{:S(2)}) async-start(), calls=%async_computation.9 | async-start | bytes 7299072 | tf_op jit(solution)/shard_map/reduce_scatter | solution.py:330
  (223 other events, 1211.9 us)
Sparse Core Ops, SparseCore 0:
  11.6 63.0 all-gather.18
  78.4 62.7 all-gather.24
  182.5 61.2 all-gather.26
  245.3 64.3 all-gather.28
  312.6 53.2 all-gather.20
  369.3 62.5 all-gather.22
  544.6 61.5 all-gather.32
  607.8 65.1 all-gather.30
  680.2 96.4 reduce-scatter.11
  847.0 92.6 reduce-scatter.9
  947.2 134.6 reduce-scatter.13
  1088.3 134.6 reduce-scatter.15
  1230.2 117.9 reduce-scatter.7
where the time goes:
time: 1370 us; the launch traced here: 1350 us
  waiting for transfers between devices  356 us (26%)
  local copies, waits for them, and re-layouts  290 us (21%)
  other arithmetic  259 us (19%)
  blocking collectives  222 us (16%)
  matrix products  210 us (15%)
  between operations  16.6 us (1%)
    select_n x64, other arithmetic, turn(): return jax.tree.map(lambda a, b: jnp.where(reached, a, b), new, before)  152 us
    reduce_scatter x1, waiting for transfers between devices, shards(): lax.psum_scatter(summed[4], ('dp', 'seq'), scatter_dimension=0, tiled=True)  141 us
    reduce_scatter x1, waiting for transfers between devices, shards(): lax.psum_scatter(summed[0], ('dp', 'seq'), scatter_dimension=0, tiled=True)  125 us
    reduce_scatter x1, waiting for transfers between devices, shards(): lax.psum_scatter(summed[3], ('dp', 'seq'), scatter_dimension=0, tiled=True)  89.8 us
    concatenate x16, local copies, waits for them, and re-layouts, features(): jnp.concatenate([jax.nn.softmax(logits, axis=-1), jax.nn.softmax(-logits,...  69.1 us
    dynamic_slice x64, local copies, waits for them, and re-layouts, turn(): part[at].astype(own.dtype)  65.5 us
    all_gather x4, blocking collectives, prefix(): lax.all_gather(part.astype(kind), axis)  62 us
    unnamed x446, local copies, waits for them, and re-layouts  59.6 us
  transfers between devices with their start and end apart: 13, of which 3 were waited for; matrix products, arithmetic and copies ran while one was open for 49% of the time, Pallas kernels for 0%

commit v1 on v0

--- a/solution.py
+++ b/solution.py
@@ -7,28 +7,103 @@
 BLOCK = 64
 
 
-def prefix(value, axis, combine, identity, reverse):
-    devices, mine = (lax.axis_size(axis), lax.axis_index(axis))
-    everything = jax.tree.map(
-        lambda part, kind: lax.all_gather(part.astype(kind), axis),
-        value,
-        (jnp.bfloat16, jnp.bfloat16),
-    )
-    start = jax.tree.map(
-        lambda part, zero: jnp.broadcast_to(jnp.asarray(zero, part.dtype), part.shape),
-        value,
-        identity,
-    )
-
-    def turn(k, before):
-        at = devices - 1 - k if reverse else k
-        reached = at > mine if reverse else at < mine
-        new = combine(
-            before, jax.tree.map(lambda part, own: part[at].astype(own.dtype), everything, value)
+AXES = ("dp", "seq")
+
+
+def grid_dims():
+    n_dp, n_seq = lax.axis_size("dp"), lax.axis_size("seq")
+    n_x = 1
+    while n_x * n_x * 4 <= n_dp:
+        n_x *= 2
+    sizes = {"y": n_dp // n_x, "x": n_x, "z": n_seq // 2, "c": 2}
+    at = lax.axis_index("dp") * n_seq + lax.axis_index("seq")
+    place = {}
+    for name in ("c", "z", "x", "y"):
+        place[name] = lax.rem(at, sizes[name])
+        at = at // sizes[name]
+    return sizes, place
+
+
+def turned(sizes, name, step):
+    pairs = []
+    for y in range(sizes["y"]):
+        for x in range(sizes["x"]):
+            for z in range(sizes["z"]):
+                for c in range(sizes["c"]):
+                    to = {"y": y, "x": x, "z": z, "c": c}
+                    to[name] = (to[name] + step) % sizes[name]
+                    flat = lambda p: ((p[0] * sizes["x"] + p[1]) * sizes["z"] + p[2]) * 2 + p[3]
+                    pairs.append((flat((y, x, z, c)), flat((to["y"], to["x"], to["z"], to["c"]))))
+    return pairs
+
+
+def send(value, sizes, name, step):
+    return lax.ppermute(value, AXES, turned(sizes, name, step))
+
+
+def gather_dim(value, grid, name):
+    sizes, place = grid
+    count = sizes[name]
+    if count == 1:
+        return value[None]
+    got = [value] + [send(value, sizes, name, k) for k in range(1, count)]
+    if count == 2:
+        low = place[name] == 0
+        return jnp.stack([jnp.where(low, got[0], got[1]), jnp.where(low, got[1], got[0])])
+    order = jnp.stack(got[::-1] + got[::-1][:-1])
+    return lax.dynamic_slice_in_dim(order, count - 1 - place[name], count, 0)
+
+
+def gather_rows(value, grid, order):
+    out = value
+    for name in order:
+        out = gather_dim(out, grid, name)
+    axes = [len(order) - 1 - order.index(name) for name in ("y", "x", "z", "c")]
+    out = jnp.transpose(out, axes + list(range(len(order), out.ndim)))
+    return out.reshape((-1,) + value.shape[1:])
+
+
+def scatter_dim(value, grid, name, axis):
+    sizes, place = grid
+    count = sizes[name]
+    mine = lax.dynamic_index_in_dim(value, place[name], axis, keepdims=False)
+    if count == 1:
+        return mine
+    total = mine.astype(jnp.float32)
+    for k in range(1, count):
+        block = lax.dynamic_index_in_dim(
+            value, lax.rem(place[name] + k, count), axis, keepdims=False
         )
-        return jax.tree.map(lambda a, b: jnp.where(reached, a, b), new, before)
-
-    return lax.fori_loop(0, devices, turn, start)
+        total = total + send(block, sizes, name, k).astype(jnp.float32)
+    return total.astype(jnp.bfloat16)
+
+
+def scatter_rows(value, grid, order):
+    sizes, _ = grid
+    names = ["y", "x", "z", "c"]
+    rows = value.shape[0] // (sizes["y"] * sizes["x"] * sizes["z"] * sizes["c"])
+    out = value.reshape(tuple(sizes[n] for n in names) + (rows,) + value.shape[1:])
+    for name in order:
+        axis = names.index(name)
+        out = scatter_dim(out, grid, name, axis)
+        names.pop(axis)
+    return out
+
+
+def prefix(value, grid, reverse):
+    sizes, place = grid
+    sign = -1 if reverse else 1
+    count = sizes["z"]
+    own = jax.tree.map(lambda v: v.astype(jnp.bfloat16), value)
+    other = jax.tree.map(lambda v: send(v, sizes, "c", 1), own)
+    total = jax.tree.map(lambda a, b: (a + b.astype(jnp.float32)).astype(jnp.bfloat16), value, other)
+    ahead = place["c"] == (0 if reverse else 1)
+    out = jax.tree.map(lambda v: jnp.where(ahead, v.astype(jnp.float32), 0.0), other)
+    for k in range(1, count):
+        got = jax.tree.map(lambda v: send(v, sizes, "z", sign * k), total)
+        valid = (place["z"] + k < count) if reverse else (place["z"] >= k)
+        out = jax.tree.map(lambda o, g: o + jnp.where(valid, g.astype(jnp.float32), 0.0), out, got)
+    return out
 
 
 def layer_norm(values, norm_gain, norm_shift):
@@ -63,10 +138,6 @@
     )
 
 
-def add_pairs(earlier, later):
-    return (earlier[0] + later[0], earlier[1] + later[1])
-
-
 def earlier_sum(values):
     zero_row = jnp.zeros_like(values[:, :1])
     return jnp.concatenate([zero_row, jnp.cumsum(values[:, :-1], axis=1)], axis=1)
@@ -76,7 +147,7 @@
     return jnp.flip(earlier_sum(jnp.flip(values, 1)), 1)
 
 
-def forward_pass(gathered, inputs, seq_count, seg_len):
+def forward_pass(grid, gathered, inputs, seq_count, seg_len):
     w_qkv, w_feat, w_out, w_fc, w_proj, gains, biases = gathered
     gains_f = gains.astype(jnp.float32)
     biases_f = biases.astype(jnp.float32)
@@ -117,13 +188,7 @@
     own_sum = jnp.sum(phi_k, axis=2, dtype=jnp.float32)
     dev_state = jnp.sum(own_state, axis=1)
     dev_sum = jnp.sum(own_sum, axis=1)
-    before_state, before_sum = prefix(
-        (dev_state, dev_sum),
-        "seq",
-        add_pairs,
-        (jnp.zeros_like(dev_state), jnp.zeros_like(dev_sum)),
-        False,
-    )
+    before_state, before_sum = prefix((dev_state, dev_sum), grid, False)
     prior_state = (before_state[:, None] + earlier_sum(own_state)).astype(jnp.bfloat16)
     prior_sum = before_sum[:, None] + earlier_sum(own_sum)
     numerator = numerator + jnp.einsum(
@@ -162,7 +227,7 @@
     return (result, saved)
 
 
-def backward_pass(gathered, saved, upstream):
+def backward_pass(grid, gathered, saved, upstream):
     w_qkv, w_feat, w_out, w_fc, w_proj, gains, biases = gathered
     (
         inputs,
@@ -225,13 +290,7 @@
     d_sum = jnp.einsum("snthf,snth->snhf", phi_q, d_denom, preferred_element_type=jnp.float32)
     dev_state = jnp.sum(d_state, axis=1)
     dev_sum = jnp.sum(d_sum, axis=1)
-    after_state, after_sum = prefix(
-        (dev_state, dev_sum),
-        "seq",
-        add_pairs,
-        (jnp.zeros_like(dev_state), jnp.zeros_like(dev_sum)),
-        True,
-    )
+    after_state, after_sum = prefix((dev_state, dev_sum), grid, True)
     d_own = (after_state[:, None] + later_sum(d_state)).astype(jnp.bfloat16)
     d_own_sum = after_sum[:, None] + later_sum(d_sum)
     d_phi_k = d_phi_k + jnp.einsum(
@@ -286,65 +345,65 @@
 
 def shards(tokens, w_qkv, w_feat, w_out, w_fc, w_proj, gains, biases, cotangent):
     micro_count, seq_count, seg_len, model_width = tokens.shape
+    grid = grid_dims()
+    low = jnp.bfloat16
+    rows = w_qkv.shape[0]
     hidden_width = w_fc.shape[1]
-    masters = (w_qkv, w_feat, w_out, w_fc, w_proj, gains, biases)
-    copies = tuple((master.astype(jnp.bfloat16) for master in masters))
-    summed = (
-        jnp.zeros((model_width, 3 * model_width), jnp.float32),
-        jnp.zeros((2, model_width, HD), jnp.float32),
-        jnp.zeros((model_width, model_width), jnp.float32),
-        jnp.zeros((model_width, hidden_width), jnp.float32),
-        jnp.zeros((hidden_width, model_width), jnp.float32),
-        jnp.zeros((2, model_width), jnp.float32),
-        jnp.zeros((11, model_width), jnp.float32),
-    )
-    results = []
-    input_grads = []
-    for micro_index in range(micro_count):
-        gathered = (
-            lax.all_gather(copies[0], ("dp", "seq"), axis=0, tiled=True),
-            lax.all_gather(copies[1], ("dp", "seq"), axis=1, tiled=True),
-            lax.all_gather(copies[2], ("dp", "seq"), axis=0, tiled=True),
-            lax.all_gather(copies[3], ("dp", "seq"), axis=0, tiled=True),
-            lax.all_gather(copies[4], ("dp", "seq"), axis=0, tiled=True),
-            lax.all_gather(copies[5], ("dp", "seq"), axis=1, tiled=True),
-            lax.all_gather(copies[6], ("dp", "seq"), axis=1, tiled=True),
-        )
-        inputs = tokens[micro_index].reshape(-1, model_width).astype(jnp.float32)
-        result, saved = forward_pass(gathered, inputs, seq_count, seg_len)
-        results.append(result.reshape(seq_count, seg_len, model_width).astype(jnp.bfloat16))
-        again = (
-            lax.all_gather(copies[0], ("dp", "seq"), axis=0, tiled=True),
-            lax.all_gather(copies[1], ("dp", "seq"), axis=1, tiled=True),
-            lax.all_gather(copies[2], ("dp", "seq"), axis=0, tiled=True),
-            lax.all_gather(copies[3], ("dp", "seq"), axis=0, tiled=True),
-            lax.all_gather(copies[4], ("dp", "seq"), axis=0, tiled=True),
-            lax.all_gather(copies[5], ("dp", "seq"), axis=1, tiled=True),
-            lax.all_gather(copies[6], ("dp", "seq"), axis=1, tiled=True),
-        )
-        upstream = cotangent[micro_index].reshape(-1, model_width).astype(jnp.float32)
-        grads, input_grad = backward_pass(again, saved, upstream)
-        input_grads.append(input_grad.reshape(seq_count, seg_len, model_width))
-        summed = tuple((held + fresh for held, fresh in zip(summed, grads)))
-    finals = (
-        lax.psum_scatter(summed[0], ("dp", "seq"), scatter_dimension=0, tiled=True),
-        lax.psum_scatter(summed[1], ("dp", "seq"), scatter_dimension=1, tiled=True),
-        lax.psum_scatter(summed[2], ("dp", "seq"), scatter_dimension=0, tiled=True),
-        lax.psum_scatter(summed[3], ("dp", "seq"), scatter_dimension=0, tiled=True),
-        lax.psum_scatter(summed[4], ("dp", "seq"), scatter_dimension=0, tiled=True),
-        lax.psum_scatter(summed[5], ("dp", "seq"), scatter_dimension=1, tiled=True),
-        lax.psum_scatter(summed[6], ("dp", "seq"), scatter_dimension=1, tiled=True),
-    )
+    first = jnp.concatenate(
+        [
+            w_qkv.astype(low),
+            jnp.transpose(w_feat, (1, 0, 2)).reshape(rows, 2 * HD).astype(low),
+            jnp.pad(jnp.concatenate([gains, biases]).T.astype(low), ((0, 0), (0, 128 - 13))),
+        ],
+        axis=1,
+    )
+    first = gather_rows(first, grid, ("z", "x", "y", "c"))
+    later = jnp.concatenate(
+        [w_fc.astype(low), w_proj.astype(low).reshape(rows, hidden_width), w_out.astype(low)],
+        axis=1,
+    )
+    later = lax.all_gather(later, AXES, axis=0, tiled=True)
+    wide = 3 * model_width
+    small = first[:, wide + 2 * HD :].T
+    gathered = (
+        first[:, :wide],
+        jnp.transpose(first[:, wide : wide + 2 * HD].reshape(model_width, 2, HD), (1, 0, 2)),
+        later[:, 2 * hidden_width :],
+        later[:, :hidden_width],
+        later[:, hidden_width : 2 * hidden_width].reshape(hidden_width, model_width),
+        small[:2],
+        small[2:13],
+    )
+    inputs = tokens.reshape(-1, model_width).astype(jnp.float32)
+    result, saved = forward_pass(grid, gathered, inputs, micro_count * seq_count, seg_len)
+    upstream = cotangent.reshape(-1, model_width).astype(jnp.float32)
+    grads, input_grad = backward_pass(grid, gathered, saved, upstream)
+    g_qkv, g_feat, g_out, g_fc, g_proj, g_gains, g_biases = grads
+    r_proj = scatter_rows(g_proj.astype(low), grid, ("c", "x", "y", "z"))
+    r_fc = scatter_rows(g_fc.astype(low), grid, ("c", "y", "x", "z"))
+    last = jnp.concatenate(
+        [
+            g_qkv.astype(low),
+            g_out.astype(low),
+            jnp.transpose(g_feat, (1, 0, 2)).reshape(model_width, 2 * HD).astype(low),
+            jnp.pad(jnp.concatenate([g_gains, g_biases]).T.astype(low), ((0, 0), (0, 128 - 13))),
+        ],
+        axis=1,
+    )
+    last = scatter_rows(last, grid, ("c", "x", "y", "z")).astype(jnp.float32)
+    small = last[:, wide + model_width + 2 * HD :].T
     return (
-        jnp.stack(results),
-        jnp.stack(input_grads),
-        finals[0],
-        finals[1],
-        finals[2],
-        finals[3],
-        finals[4],
-        finals[5],
-        finals[6],
+        result.reshape(tokens.shape).astype(low),
+        input_grad.reshape(tokens.shape),
+        last[:, :wide],
+        jnp.transpose(
+            last[:, wide + model_width : wide + model_width + 2 * HD].reshape(rows, 2, HD), (1, 0, 2)
+        ),
+        last[:, wide : wide + model_width],
+        r_fc.astype(jnp.float32),
+        r_proj.astype(jnp.float32),
+        small[:2],
+        small[2:13],
     )
 
 

time: 1370 us -> 935 us (0.68)
  blocking collectives: 222 us -> 0 us
  other arithmetic: 259 us -> 111 us
  starting transfers between devices: 1.54 us -> 107 us
  local copies, waits for them, and re-layouts: 290 us -> 218 us
  waiting for transfers between devices: 356 us -> 306 us
  matrix products: 210 us -> 170 us
    reduce_scatter x5 -> x0, waiting for transfers between devices: 356 us -> none  [the longest x1 141 us: shards(): lax.psum_scatter(summed[4], ('dp', 'seq'), scatter_dimension=0, tiled=True)]
    ppermute x0 -> x40, waiting for transfers between devices: none -> 306 us  [send(): return lax.ppermute(value, AXES, turned(sizes, name, step))]
    all_gather x7 -> x0, blocking collectives: 183 us -> none  [the longest x4 62 us: prefix(): lax.all_gather(part.astype(kind), axis)]
    select_n x64 -> x0, other arithmetic: 152 us -> none  [turn(): return jax.tree.map(lambda a, b: jnp.where(reached, a, b), new, before)]
    ppermute x0 -> x40, starting transfers between devices: none -> 107 us  [send(): return lax.ppermute(value, AXES, turned(sizes, name, step))]
    dynamic_slice x64 -> x3, local copies, waits for them, and re-layouts: 65.5 us -> 5.78 us  [the longest x1 4.12 us: scatter_dim(): mine = lax.dynamic_index_in_dim(value, place[name], axis, keepdims=False)]
    unnamed x1 -> x0, blocking collectives: 38.3 us -> none
    convert_element_type x5 -> x28, other arithmetic: 5.6 us -> 24.1 us  [the longest x9 10.1 us: scatter_dim(): return total.astype(jnp.bfloat16)]
  transfers between devices with their start and end apart: 13 -> 41, of which waited for: 3 -> 15; matrix products, arithmetic and copies ran while one was open for 49% -> 38% of each run, Pallas kernels for 0% -> 0%
where the time goes in v1:
time: 935 us; the launch traced here: 928 us
  waiting for transfers between devices  306 us (33%)
  local copies, waits for them, and re-layouts  218 us (23%)
  matrix products  170 us (18%)
  other arithmetic  111 us (12%)
  starting transfers between devices  107 us (11%)
  between operations  15.9 us (2%)
    ppermute x40, waiting for transfers between devices, send(): return lax.ppermute(value, AXES, turned(sizes, name, step))  306 us
    ppermute x40, starting transfers between devices, send(): return lax.ppermute(value, AXES, turned(sizes, name, step))  107 us
    concatenate x8, local copies, waits for them, and re-layouts, features(): jnp.concatenate([jax.nn.softmax(logits, axis=-1), jax.nn.softmax(-logits,...  62.7 us
    unnamed x260, local copies, waits for them, and re-layouts  42.6 us
    dot_general x4, matrix products, dot_second(): lax.dot_general(first_op, second_op, (((1,), (1,)), ((), ())), preferred_...  37.9 us
    dot_general x4, matrix products, dot_first(): lax.dot_general(first_op, second_op, (((0,), (0,)), ((), ())), preferred_...  33.3 us
    dot_general x4, matrix products, dot_plain(): return jnp.dot(first_op, second_op, preferred_element_type=jnp.float32)  32.4 us
  transfers between devices with their start and end apart: 41, of which 15 were waited for; matrix products, arithmetic and copies ran while one was open for 38% of the time, Pallas kernels for 0%

profile of v1, /device:TPU:0, one launch (start us, length us, event | category | flops | bytes accessed | tf_op | source)
XLA Modules:
  0.0 927.6 jit_solution(14135573135174539556)
XLA Ops:
  26.0 13.9 %collective-permute-done.3 = bf16[4,24,2560]{2,1,0:T(8,128)(2,1)S(1)} collective-permute-done((bf16[4,24,2560]{2,1,0:T(8,128)(2,1)S(1)}, bf16[4,24,2560]{2,1,0:T(8,128)(2,1)S(1)}, u32[]{:S(2)}, u32[]{:S(2)}) %collective-permute-start.3) | collective-permute-done | bytes 491552 | tf_op jit(solution)/shard_map/ppermute | solution.py:41
  42.6 26.4 %collective-permute-done.4 = bf16[2,4,24,2560]{3,2,1,0:T(8,128)(2,1)} collective-permute-done((bf16[2,4,24,2560]{3,2,1,0:T(8,128)(2,1)}, bf16[2,4,24,2560]{3,2,1,0:T(8,128)(2,1)}, u32[]{:S(2)}, u32[]{:S(2)}) %collective-permute-start.4) | collective-permute-done | bytes 983072 | tf_op jit(solution)/shard_map/ppermute | solution.py:41
  114.2 8.7 copy.170
  135.8 8.7 copy.171
  157.3 8.7 copy.174
  178.9 8.7 copy.175
  229.6 126.7 %collective-permute-done.12 = bf16[8,12,128]{2,1,0:T(8,128)(2,1)} collective-permute-done((bf16[8,12,128]{2,1,0:T(8,128)(2,1)}, bf16[8,12,128]{2,1,0:T(8,128)(2,1)}, u32[]{:S(2)}, u32[]{:S(2)}) %collective-permute-start.12) | collective-permute-done | bytes 24608 | tf_op jit(solution)/shard_map/ppermute | solution.py:41
  377.8 8.0 convert_element_type.425
  390.7 8.5 reshape.291
  403.7 11.3 %fusion.21 = f32[1024,3072]{1,0:T(8,128)} fusion(bf16[768,6912]{1,0:T(8,128)(2,1)} %all-gather.2.cloned.1.call-done, f32[1024,768]{1,0:T(8,128)S(1)} %get-tuple-element.112, f32[768]{0:T(1024)S(1)} %get-tuple-element.56, f32[768]{0:T(1024)S(1)} %get-tuple-element.120, f32[1024]{0:T(1024)S(1)} %fusion.110, f32[1024]{0:T(1024)S(1)} %broadcast_multiply_fusion), kind=kOutput, calls=%fused_computation.50 | convolution fusion | flops 4835770368 | bytes 20461568 | tf_op jit(solution)/shard_map/dot_general | solution.py:126
  415.0 12.6 %convolution_convert_fusion = bf16[3072,768]{1,0:T(8,128)(2,1)} fusion(bf16[1024,768]{1,0:T(8,128)(2,1)S(1)} %bitcast.347, f32[1024,3072]{1,0:T(8,128)} %fusion.21, f32[3072]{0:T(1024)S(1)} %copy-done.99), kind=kOutput, calls=%fused_computation.38 | convolution fusion | flops 4865654784 | bytes 18886656 | tf_op jit(solution)/shard_map/dot_general | solution.py:130
  427.6 16.9 %fusion.132 = (bf16[3072]{0:T(1024)(128)(2,1)}, bf16[1024,3072]{1,0:T(8,128)(2,1)}) fusion(f32[1024,3072]{1,0:T(8,128)} %fusion.21, f32[3072]{0:T(1024)S(1)} %copy-done.99, bf16[3072,768]{1,0:T(8,128)(2,1)S(1)} %bitcast.365, bf16[1024,768]{1,0:T(8,128)(2,1)S(1)} %bitcast.348), kind=kOutput, calls=%fused_computation.278 | convolution fusion | flops 4901041152 | bytes 25184256 | tf_op jit(solution)/shard_map/dot_general | solution.py:136
  444.6 9.9 %convolution_convert_fusion.1 = bf16[768,3072]{1,0:T(8,128)(2,1)} fusion(bf16[1024,3072]{1,0:T(8,128)(2,1)} %get-tuple-element.118, f32[1024,768]{1,0:T(8,128)S(1)} %get-tuple-element.112, f32[768]{0:T(1024)S(1)} %get-tuple-element.56, f32[768]{0:T(1024)S(1)} %get-tuple-element.120, f32[1024]{0:T(1024)S(1)} %fusion.110, f32[1024]{0:T(1024)S(1)} %broadcast_multiply_fusion), kind=kOutput, calls=%fused_computation.39 | convolution fusion | flops 4838129664 | bytes 14170112 | tf_op jit(solution)/shard_map/dot_general | solution.py:130
  454.5 8.8 multiply_reduce_fusion.1
  493.6 13.0 %add_convert_fusion.6 = bf16[1024,768]{1,0:T(8,128)(2,1)} fusion(f32[1024,768]{1,0:T(8,128)S(1)} %copy-done.34, bf16[3072,768]{1,0:T(8,128)(2,1)S(1)} %bitcast.367, f32[768]{0:T(1024)S(1)} %copy-done.104, f32[1024,3072]{1,0:T(8,128)} %fusion.21, f32[3072]{0:T(1024)S(1)} %copy-done.100), kind=kOutput, calls=%fused_computation.104 | convolution fusion | flops 4865654784 | bytes 22035456 | tf_op jit(solution)/shard_map/dot_general | solution.py:126
  532.0 10.9 %fusion.120 = (f32[1024,12,64]{2,0,1:T(8,128)}, f32[1024,12,64]{2,0,1:T(8,128)}) fusion(f32[1024,12,128]{2,0,1:T(8,128)} %bitcast.331), kind=kLoop, calls=%fused_computation.266 | loop fusion | bytes 12582912 | tf_op jit(solution)/shard_map/transpose(jvp())/split | solution.py:116
  608.0 23.6 %collective-permute-done.17 = bf16[8,12,128,64]{2,3,1,0:T(8,128)(2,1)S(1)} collective-permute-done((bf16[8,12,128,64]{2,3,1,0:T(8,128)(2,1)S(1)}, bf16[8,12,128,64]{2,3,1,0:T(8,128)(2,1)S(1)}, u32[]{:S(2)}, u32[]{:S(2)}) %collective-permute-start.17) | collective-permute-done | bytes 1572896 | tf_op jit(solution)/shard_map/ppermute | solution.py:41
  631.6 66.0 %collective-permute-done.16 = bf16[8,12,128,64]{2,3,1,0:T(8,128)(2,1)S(1)} collective-permute-done((bf16[8,12,128,64]{2,3,1,0:T(8,128)(2,1)S(1)}, bf16[8,12,128,64]{2,3,1,0:T(8,128)(2,1)S(1)}, u32[]{:S(2)}, u32[]{:S(2)}) %collective-permute-start.16) | collective-permute-done | bytes 1572896 | tf_op jit(solution)/shard_map/ppermute | solution.py:41
  754.0 8.4 reshape.298
  762.5 9.1 fusion.116
  773.0 8.4 convolution_convert_fusion.2
  797.6 21.6 %collective-permute-done.29 = bf16[2,4,24,3072]{3,2,1,0:T(8,128)(2,1)S(1)} collective-permute-done((bf16[2,4,24,3072]{3,2,1,0:T(8,128)(2,1)S(1)}, bf16[2,4,24,3072]{3,2,1,0:T(8,128)(2,1)S(1)}, u32[]{:S(2)}, u32[]{:S(2)}) %collective-permute-start.29) | collective-permute-done | bytes 1179680 | tf_op jit(solution)/shard_map/ppermute | solution.py:41
  830.2 33.7 %collective-permute-start.37 = (bf16[96,768]{1,0:T(8,128)(2,1)S(1)}, bf16[96,768]{1,0:T(8,128)(2,1)S(1)}, u32[]{:S(2)}, u32[]{:S(2)}) collective-permute-start(bf16[96,768]{1,0:T(8,128)(2,1)S(1)} %get-tuple-element.87), channel_id=1, source_target_pairs={{0,2},{1,3},{2,4},{3,5},{4,6},{5,7},{6,0},{7,1},{8,10},{9,11},{10,... | collective-permute-start | bytes 442376 | tf_op jit(solution)/shard_map/ppermute | solution.py:41
  870.7 20.9 %collective-permute-start.32 = (bf16[24,3072]{1,0:T(8,128)(2,1)S(1)}, bf16[24,3072]{1,0:T(8,128)(2,1)S(1)}, u32[]{:S(2)}, u32[]{:S(2)}) collective-permute-start(bf16[24,3072]{1,0:T(8,128)(2,1)S(1)} %get-tuple-element.92), channel_id=1, source_target_pairs={{0,4},{1,5},{2,6},{3,7},{4,0},{5,1},{6,2},{7,3},{8,12},{9,13},{10,... | collective-permute-start | bytes 442376 | tf_op jit(solution)/shard_map/ppermute | solution.py:41
  (534 shorter events, 418.2 us)
Async XLA Ops:
  7.2 378.7 %all-gather.2.cloned.1.call-start = ((), (), s32[]{:S(2)}) async-start(), calls=%async_computation | async-start | bytes 10948608 | tf_op jit(solution)/shard_map/all_gather | solution.py:365
  41.1 27.9 %collective-permute-start.4 = (bf16[2,4,24,2560]{3,2,1,0:T(8,128)(2,1)}, bf16[2,4,24,2560]{3,2,1,0:T(8,128)(2,1)}, u32[]{:S(2)}, u32[]{:S(2)}) collective-permute-start(bf16[2,4,24,2560]{3,2,1,0:T(8,128)(2,1)} %pad_maximum_fusion.5), channel_id=1, source_target_pairs={{0,16},{1,17},{2,18},{3,19},{4,20},{5,21},{6,22},{7,23},{8,24},{9,... | collective-permute-start | bytes 2949128 | tf_op jit(solution)/shard_map/ppermute | solution.py:41
  213.1 145.8 %collective-permute-start.9 = (bf16[8,12,128,64]{2,3,1,0:T(8,128)(2,1)}, bf16[8,12,128,64]{2,3,1,0:T(8,128)(2,1)}, u32[]{:S(2)}, u32[]{:S(2)}) collective-permute-start(bf16[8,12,128,64]{2,3,1,0:T(8,128)(2,1)} %fusion.26), channel_id=1, source_target_pairs={{0,6},{1,7},{2,0},{3,1},{4,2},{5,3},{6,4},{7,5},{8,14},{9,15},{10,... | collective-permute-start | bytes 4718600 | tf_op jit(solution)/shard_map/ppermute | solution.py:41
  214.7 144.2 %collective-permute-start.8 = (bf16[8,12,128,64]{2,3,1,0:T(8,128)(2,1)}, bf16[8,12,128,64]{2,3,1,0:T(8,128)(2,1)}, u32[]{:S(2)}, u32[]{:S(2)}) collective-permute-start(bf16[8,12,128,64]{2,3,1,0:T(8,128)(2,1)} %fusion.26), channel_id=1, source_target_pairs={{0,4},{1,5},{2,6},{3,7},{4,0},{5,1},{6,2},{7,3},{8,12},{9,13},{10,... | collective-permute-start | bytes 4718600 | tf_op jit(solution)/shard_map/ppermute | solution.py:41
  218.2 141.3 %collective-permute-start.7 = (bf16[8,12,128,64]{2,3,1,0:T(8,128)(2,1)}, bf16[8,12,128,64]{2,3,1,0:T(8,128)(2,1)}, u32[]{:S(2)}, u32[]{:S(2)}) collective-permute-start(bf16[8,12,128,64]{2,3,1,0:T(8,128)(2,1)} %fusion.26), channel_id=1, source_target_pairs={{0,2},{1,3},{2,4},{3,5},{4,6},{5,7},{6,0},{7,1},{8,10},{9,11},{10,... | collective-permute-start | bytes 4718600 | tf_op jit(solution)/shard_map/ppermute | solution.py:41
  220.8 135.5 %collective-permute-start.12 = (bf16[8,12,128]{2,1,0:T(8,128)(2,1)}, bf16[8,12,128]{2,1,0:T(8,128)(2,1)}, u32[]{:S(2)}, u32[]{:S(2)}) collective-permute-start(bf16[8,12,128]{2,1,0:T(8,128)(2,1)} %fusion.103), channel_id=1, source_target_pairs={{0,4},{1,5},{2,6},{3,7},{4,0},{5,1},{6,2},{7,3},{8,12},{9,13},{10,... | collective-permute-start | bytes 73736 | tf_op jit(solution)/shard_map/ppermute | solution.py:41
  220.9 135.4 %collective-permute-start.11 = (bf16[8,12,128]{2,1,0:T(8,128)(2,1)}, bf16[8,12,128]{2,1,0:T(8,128)(2,1)}, u32[]{:S(2)}, u32[]{:S(2)}) collective-permute-start(bf16[8,12,128]{2,1,0:T(8,128)(2,1)} %fusion.103), channel_id=1, source_target_pairs={{0,2},{1,3},{2,4},{3,5},{4,6},{5,7},{6,0},{7,1},{8,10},{9,11},{10,... | collective-permute-start | bytes 73736 | tf_op jit(solution)/shard_map/ppermute | solution.py:41
  512.3 86.2 %collective-permute-start.34 = (bf16[2,2,4,96,768]{4,3,2,0,1:T(8,128)(2,1)}, bf16[2,2,4,96,768]{4,3,2,0,1:T(8,128)(2,1)}, u32[]{:S(2)}, u32[]{:S(2)}) collective-permute-start(bf16[2,2,4,96,768]{4,3,2,0,1:T(8,128)(2,1)} %bitcast.327), channel_id=1, source_target_pairs={{0,1},{1,0},{2,3},{3,2},{4,5},{5,4},{6,7},{7,6},{8,9},{9,8},{10,11... | collective-permute-start | bytes 7077896 | tf_op jit(solution)/shard_map/ppermute | solution.py:41
  514.0 89.8 %collective-permute-start.28 = (bf16[2,2,4,24,3072]{4,3,2,1,0:T(8,128)(2,1)}, bf16[2,2,4,24,3072]{4,3,2,1,0:T(8,128)(2,1)}, u32[]{:S(2)}, u32[]{:S(2)}) collective-permute-start(bf16[2,2,4,24,3072]{4,3,2,1,0:T(8,128)(2,1)} %dynamic-slice_bitcast_fusion.1), channel_id=1, source_target_pairs={{0,1},{1,0},{2,3},{3,2},{4,5},{5,4},{6,7},{7,6},{8,9},{9,8},{10,11... | collective-permute-start | bytes 7077896 | tf_op jit(solution)/shard_map/ppermute | solution.py:41
  516.0 69.6 %collective-permute-start.18 = (bf16[8,12,128]{2,1,0:T(8,128)(2,1)}, bf16[8,12,128]{2,1,0:T(8,128)(2,1)}, u32[]{:S(2)}, u32[]{:S(2)}) collective-permute-start(bf16[8,12,128]{2,1,0:T(8,128)(2,1)} %convert_element_type.446), channel_id=1, source_target_pairs={{0,1},{1,0},{2,3},{3,2},{4,5},{5,4},{6,7},{7,6},{8,9},{9,8},{10,11... | collective-permute-start | bytes 73736 | tf_op jit(solution)/shard_map/ppermute | solution.py:41
  531.5 55.3 %collective-permute-start.14 = (bf16[8,12,128,64]{2,3,1,0:T(8,128)(2,1)}, bf16[8,12,128,64]{2,3,1,0:T(8,128)(2,1)}, u32[]{:S(2)}, u32[]{:S(2)}) collective-permute-start(bf16[8,12,128,64]{2,3,1,0:T(8,128)(2,1)} %convert_element_type.439), channel_id=1, source_target_pairs={{0,1},{1,0},{2,3},{3,2},{4,5},{5,4},{6,7},{7,6},{8,9},{9,8},{10,11... | collective-permute-start | bytes 4718600 | tf_op jit(solution)/shard_map/ppermute | solution.py:41
  592.4 39.3 %collective-permute-start.17 = (bf16[8,12,128,64]{2,3,1,0:T(8,128)(2,1)S(1)}, bf16[8,12,128,64]{2,3,1,0:T(8,128)(2,1)S(1)}, u32[]{:S(2)}, u32[]{:S(2)}) collective-permute-start(bf16[8,12,128,64]{2,3,1,0:T(8,128)(2,1)S(1)} %fusion.30), channel_id=1, source_target_pairs={{0,2},{1,3},{2,4},{3,5},{4,6},{5,7},{6,0},{7,1},{8,10},{9,11},{10,... | collective-permute-start | bytes 4718600 | tf_op jit(solution)/shard_map/ppermute | solution.py:41
  593.0 104.7 %collective-permute-start.16 = (bf16[8,12,128,64]{2,3,1,0:T(8,128)(2,1)S(1)}, bf16[8,12,128,64]{2,3,1,0:T(8,128)(2,1)S(1)}, u32[]{:S(2)}, u32[]{:S(2)}) collective-permute-start(bf16[8,12,128,64]{2,3,1,0:T(8,128)(2,1)S(1)} %fusion.30), channel_id=1, source_target_pairs={{0,4},{1,5},{2,6},{3,7},{4,0},{5,1},{6,2},{7,3},{8,12},{9,13},{10,... | collective-permute-start | bytes 4718600 | tf_op jit(solution)/shard_map/ppermute | solution.py:41
  594.5 103.1 %collective-permute-start.15 = (bf16[8,12,128,64]{2,3,1,0:T(8,128)(2,1)S(1)}, bf16[8,12,128,64]{2,3,1,0:T(8,128)(2,1)S(1)}, u32[]{:S(2)}, u32[]{:S(2)}) collective-permute-start(bf16[8,12,128,64]{2,3,1,0:T(8,128)(2,1)S(1)} %fusion.30), channel_id=1, source_target_pairs={{0,6},{1,7},{2,0},{3,1},{4,2},{5,3},{6,4},{7,5},{8,14},{9,15},{10,... | collective-permute-start | bytes 4718600 | tf_op jit(solution)/shard_map/ppermute | solution.py:41
  602.3 192.4 %collective-permute-start.35 = (bf16[2,4,96,768]{3,2,1,0:T(8,128)(2,1)}, bf16[2,4,96,768]{3,2,1,0:T(8,128)(2,1)}, u32[]{:S(2)}, u32[]{:S(2)}) collective-permute-start(bf16[2,4,96,768]{3,2,1,0:T(8,128)(2,1)} %dynamic-slice_bitcast_fusion.3), channel_id=1, source_target_pairs={{0,8},{1,9},{2,10},{3,11},{4,12},{5,13},{6,14},{7,15},{8,0},{9,1},... | collective-permute-start | bytes 3538952 | tf_op jit(solution)/shard_map/ppermute | solution.py:41
  788.8 32.5 %collective-permute-start.22 = (bf16[2,2,4,24,3328]{4,3,2,1,0:T(8,128)(2,1)S(1)}, bf16[2,2,4,24,3328]{4,3,2,1,0:T(8,128)(2,1)S(1)}, u32[]{:S(2)}, u32[]{:S(2)}) collective-permute-start(bf16[2,2,4,24,3328]{4,3,2,1,0:T(8,128)(2,1)S(1)} %dynamic-slice_bitcast_fusion), channel_id=1, source_target_pairs={{0,1},{1,0},{2,3},{3,2},{4,5},{5,4},{6,7},{7,6},{8,9},{9,8},{10,11... | collective-permute-start | bytes 7667720 | tf_op jit(solution)/shard_map/ppermute | solution.py:41
  790.3 29.0 %collective-permute-start.29 = (bf16[2,4,24,3072]{3,2,1,0:T(8,128)(2,1)S(1)}, bf16[2,4,24,3072]{3,2,1,0:T(8,128)(2,1)S(1)}, u32[]{:S(2)}, u32[]{:S(2)}) collective-permute-start(bf16[2,4,24,3072]{3,2,1,0:T(8,128)(2,1)S(1)} %dynamic-slice_bitcast_fusion.4), channel_id=1, source_target_pairs={{0,16},{1,17},{2,18},{3,19},{4,20},{5,21},{6,22},{7,23},{8,24},{9,... | collective-permute-start | bytes 3538952 | tf_op jit(solution)/shard_map/ppermute | solution.py:41
  796.3 33.7 %collective-permute-start.36 = (bf16[4,96,768]{2,1,0:T(8,128)(2,1)S(1)}, bf16[4,96,768]{2,1,0:T(8,128)(2,1)S(1)}, u32[]{:S(2)}, u32[]{:S(2)}) collective-permute-start(bf16[4,96,768]{2,1,0:T(8,128)(2,1)S(1)} %dynamic-slice_bitcast_fusion.6), channel_id=1, source_target_pairs={{0,16},{1,17},{2,18},{3,19},{4,20},{5,21},{6,22},{7,23},{8,24},{9,... | collective-permute-start | bytes 1769480 | tf_op jit(solution)/shard_map/ppermute | solution.py:41
  819.7 45.0 %collective-permute-start.30 = (bf16[4,24,3072]{2,1,0:T(8,128)(2,1)S(1)}, bf16[4,24,3072]{2,1,0:T(8,128)(2,1)S(1)}, u32[]{:S(2)}, u32[]{:S(2)}) collective-permute-start(bf16[4,24,3072]{2,1,0:T(8,128)(2,1)S(1)} %dynamic-slice_bitcast_fusion.7), channel_id=1, source_target_pairs={{0,8},{1,9},{2,10},{3,11},{4,12},{5,13},{6,14},{7,15},{8,0},{9,1},... | collective-permute-start | bytes 1769480 | tf_op jit(solution)/shard_map/ppermute | solution.py:41
  822.0 48.7 %collective-permute-start.23 = (bf16[2,4,24,3328]{3,2,1,0:T(8,128)(2,1)S(1)}, bf16[2,4,24,3328]{3,2,1,0:T(8,128)(2,1)S(1)}, u32[]{:S(2)}, u32[]{:S(2)}) collective-permute-start(bf16[2,4,24,3328]{3,2,1,0:T(8,128)(2,1)S(1)} %dynamic-slice_bitcast_fusion.2), channel_id=1, source_target_pairs={{0,8},{1,9},{2,10},{3,11},{4,12},{5,13},{6,14},{7,15},{8,0},{9,1},... | collective-permute-start | bytes 3833864 | tf_op jit(solution)/shard_map/ppermute | solution.py:41
  830.2 77.9 %collective-permute-start.37 = (bf16[96,768]{1,0:T(8,128)(2,1)S(1)}, bf16[96,768]{1,0:T(8,128)(2,1)S(1)}, u32[]{:S(2)}, u32[]{:S(2)}) collective-permute-start(bf16[96,768]{1,0:T(8,128)(2,1)S(1)} %get-tuple-element.87), channel_id=1, source_target_pairs={{0,2},{1,3},{2,4},{3,5},{4,6},{5,7},{6,0},{7,1},{8,10},{9,11},{10,... | collective-permute-start | bytes 442376 | tf_op jit(solution)/shard_map/ppermute | solution.py:41
  864.0 45.4 %collective-permute-start.39 = (bf16[96,768]{1,0:T(8,128)(2,1)S(1)}, bf16[96,768]{1,0:T(8,128)(2,1)S(1)}, u32[]{:S(2)}, u32[]{:S(2)}) collective-permute-start(bf16[96,768]{1,0:T(8,128)(2,1)S(1)} %get-tuple-element.88), channel_id=1, source_target_pairs={{0,6},{1,7},{2,0},{3,1},{4,2},{5,3},{6,4},{7,5},{8,14},{9,15},{10,... | collective-permute-start | bytes 442376 | tf_op jit(solution)/shard_map/ppermute | solution.py:41
  864.9 27.1 %collective-permute-start.31 = (bf16[24,3072]{1,0:T(8,128)(2,1)S(1)}, bf16[24,3072]{1,0:T(8,128)(2,1)S(1)}, u32[]{:S(2)}, u32[]{:S(2)}) collective-permute-start(bf16[24,3072]{1,0:T(8,128)(2,1)S(1)} %get-tuple-element.90), channel_id=1, source_target_pairs={{0,2},{1,3},{2,4},{3,5},{4,6},{5,7},{6,0},{7,1},{8,10},{9,11},{10,... | collective-permute-start | bytes 442376 | tf_op jit(solution)/shard_map/ppermute | solution.py:41
  870.7 29.8 %collective-permute-start.32 = (bf16[24,3072]{1,0:T(8,128)(2,1)S(1)}, bf16[24,3072]{1,0:T(8,128)(2,1)S(1)}, u32[]{:S(2)}, u32[]{:S(2)}) collective-permute-start(bf16[24,3072]{1,0:T(8,128)(2,1)S(1)} %get-tuple-element.92), channel_id=1, source_target_pairs={{0,4},{1,5},{2,6},{3,7},{4,0},{5,1},{6,2},{7,3},{8,12},{9,13},{10,... | collective-permute-start | bytes 442376 | tf_op jit(solution)/shard_map/ppermute | solution.py:41
  (141 other events, 1867.6 us)
Sparse Core Ops, SparseCore 0:
  21.4 88.9 all-gather.1

commit v2 on v1

v2 whole, which is shorter than its diff:
```python
import functools

import jax
import jax.numpy as jnp
from jax import lax
from jax.experimental import pallas as pl
from jax.experimental.pallas import tpu as pltpu
from jax.sharding import PartitionSpec as P

HD = 64
PAIR = 2 * HD
AXES = ("dp", "seq")
LOW = jnp.bfloat16
F32 = jnp.float32
VMEM_BYTES = 60 * 1024 * 1024
ZROWS = 16

def grid_dims():
    n_dp, n_seq = lax.axis_size("dp"), lax.axis_size("seq")
    n_x = 1
    while n_x * n_x * 4 <= n_dp:
        n_x *= 2
    sizes = {"y": n_dp // n_x, "x": n_x, "z": n_seq // 2, "c": 2}
    at = lax.axis_index("dp") * n_seq + lax.axis_index("seq")
    place = {}
    for name in ("c", "z", "x", "y"):
        place[name] = lax.rem(at, sizes[name])
        at = at // sizes[name]
    return sizes, place


def turned(sizes, name, step):
    pairs = []
    for y in range(sizes["y"]):
        for x in range(sizes["x"]):
            for z in range(sizes["z"]):
                for c in range(sizes["c"]):
                    to = {"y": y, "x": x, "z": z, "c": c}
                    to[name] = (to[name] + step) % sizes[name]
                    flat = lambda p: ((p[0] * sizes["x"] + p[1]) * sizes["z"] + p[2]) * 2 + p[3]
                    pairs.append((flat((y, x, z, c)), flat((to["y"], to["x"], to["z"], to["c"]))))
    return pairs


def send(value, sizes, name, step):
    return lax.ppermute(value, AXES, turned(sizes, name, step))


def gather_dim(value, grid, name):
    sizes, place = grid
    count = sizes[name]
    if count == 1:
        return value[None]
    got = [value] + [send(value, sizes, name, k) for k in range(1, count)]
    if count == 2:
        low = place[name] == 0
        return jnp.stack([jnp.where(low, got[0], got[1]), jnp.where(low, got[1], got[0])])
    order = jnp.stack(got[::-1] + got[::-1][:-1])
    return lax.dynamic_slice_in_dim(order, count - 1 - place[name], count, 0)


def gather_rows(value, grid, order):
    out = value
    for name in order:
        out = gather_dim(out, grid, name)
    axes = [len(order) - 1 - order.index(name) for name in ("y", "x", "z", "c")]
    out = jnp.transpose(out, axes + list(range(len(order), out.ndim)))
    return out.reshape((-1,) + value.shape[1:])


def scatter_dim(value, grid, name, axis):
    sizes, place = grid
    count = sizes[name]
    mine = lax.dynamic_index_in_dim(value, place[name], axis, keepdims=False)
    if count == 1:
        return mine
    total = mine.astype(F32)
    for k in range(1, count):
        block = lax.dynamic_index_in_dim(
            value, lax.rem(place[name] + k, count), axis, keepdims=False
        )
        total = total + send(block, sizes, name, k).astype(F32)
    return total.astype(LOW)


def scatter_rows(value, grid, order):
    sizes, _ = grid
    names = ["y", "x", "z", "c"]
    rows = value.shape[0] // (sizes["y"] * sizes["x"] * sizes["z"] * sizes["c"])
    out = value.reshape(tuple(sizes[n] for n in names) + (rows,) + value.shape[1:])
    for name in order:
        axis = names.index(name)
        out = scatter_dim(out, grid, name, axis)
        names.pop(axis)
    return out


def moved(sizes, name, step):
    pairs = turned(sizes, name, step)
    span = 2
    return [
        (a, b)
        for a, b in pairs
        if 0 <= (a // span) % sizes["z"] + step < sizes["z"]
    ]


def prefix(own, grid, reverse):
    sizes, place = grid
    sign = -1 if reverse else 1
    half = own.shape[0] // 2
    other = send(own, sizes, "c", 1)
    first = place["c"] * half
    mine = lax.dynamic_slice_in_dim(own, first, half, 0).astype(F32)
    mine = (mine + lax.dynamic_slice_in_dim(other, first, half, 0).astype(F32)).astype(LOW)
    total = 0.0
    for k in range(1, sizes["z"]):
        total = total + lax.ppermute(mine, AXES, moved(sizes, "z", sign * k)).astype(F32)
    total = total.astype(LOW)
    theirs = send(total, sizes, "c", 1)
    low = place["c"] == 0
    both = jnp.concatenate([jnp.where(low, total, theirs), jnp.where(low, theirs, total)])
    ahead = place["c"] == (0 if reverse else 1)
    return (both.astype(F32) + jnp.where(ahead, other.astype(F32), 0.0)).astype(LOW)


def dot(a, b):
    return jnp.dot(a, b, preferred_element_type=F32)


def dot_nt(a, b):
    return lax.dot_general(a, b, (((1,), (1,)), ((), ())), preferred_element_type=F32)


def dot_tn(a, b):
    return lax.dot_general(a, b, (((0,), (0,)), ((), ())), preferred_element_type=F32)


def normed(values):
    centred = values - jnp.mean(values, axis=-1, keepdims=True)
    spread = jnp.mean(centred * centred, axis=-1, keepdims=True)
    scale = lax.rsqrt(spread + 1e-05)
    return centred * scale, scale


def norm_back(grad, gain, unit, scale):
    eg = grad * gain
    inner = eg - jnp.mean(eg, axis=-1, keepdims=True)
    return scale * (inner - unit * jnp.mean(eg * unit, axis=-1, keepdims=True))


def lanes(shape=(PAIR, PAIR)):
    return lax.broadcasted_iota(jnp.int32, shape, 1)


def subs(shape=(PAIR, PAIR)):
    return lax.broadcasted_iota(jnp.int32, shape, 0)


def soft_pair(logits):
    high = jnp.max(logits, axis=0, keepdims=True)
    small = jnp.min(logits, axis=0, keepdims=True)
    e1 = jnp.exp(logits - high)
    e2 = jnp.exp(small - logits)
    p1 = e1 * (1.0 / jnp.sum(e1, axis=0, keepdims=True))
    p2 = e2 * (1.0 / jnp.sum(e2, axis=0, keepdims=True))
    return jnp.concatenate([p1, p2], axis=0)


def soft_back(phi, grad):
    prod = phi * grad
    s1 = jnp.sum(prod[:HD], axis=0, keepdims=True)
    s2 = jnp.sum(prod[HD:], axis=0, keepdims=True)
    return (prod[:HD] - phi[:HD] * s1) - (prod[HD:] - phi[HD:] * s2)


def enter_kernel(x_ref, w_ref, maps_ref, vec_ref, hid_ref, qkv_ref, pq_ref, pk_ref, st_ref):
    width = x_ref.shape[1]
    seqs = pq_ref.shape[0]
    heads = pq_ref.shape[1]
    unit, _ = normed(x_ref[...].astype(F32))
    hid_ref[...] = (unit * vec_ref[0:1, :] + vec_ref[2:3, :]).astype(LOW)
    for part in range(3):
        span = slice(part * width, (part + 1) * width)
        qkv_ref[:, span] = (dot(hid_ref[...], w_ref[:, span]) + vec_ref[3 + part : 4 + part, :]).astype(LOW)

    def one(s, carry):
        rows = pl.ds(pl.multiple_of(s * PAIR, PAIR), PAIR)
        lane = lanes()
        cols = jnp.zeros((PAIR, PAIR), F32)
        for p in range(heads // 2):
            at = slice(p * PAIR, (p + 1) * PAIR)
            for which, ref in ((0, pq_ref), (1, pk_ref)):
                value = qkv_ref[rows, which * width + p * PAIR : which * width + (p + 1) * PAIR]
                logits = dot_nt(maps_ref[which, p], value)
                ref[s, 2 * p] = soft_pair(logits[:HD]).astype(LOW)
                ref[s, 2 * p + 1] = soft_pair(logits[HD:]).astype(LOW)
            value = qkv_ref[rows, 2 * width + p * PAIR : 2 * width + (p + 1) * PAIR]
            own = []
            for h in (2 * p, 2 * p + 1):
                keys = pk_ref[s, h]
                own.append(dot(keys, value))
                cols = jnp.where(lane == h, jnp.sum(keys.astype(F32), axis=1, keepdims=True), cols)
            st_ref[s, at, :] = jnp.where(lane < HD, own[0], own[1]).astype(LOW)
        st_ref[s, width : width + ZROWS, :] = cols.T[:ZROWS].astype(LOW)
        return carry

    lax.fori_loop(0, seqs, one, 0)


def middle_kernel(
    x_ref, dy_ref, v_ref, pq_ref, pk_ref, pri_ref, w_ref, vec_ref, *rest
):
    (out_ref, a_ref, h2_ref, g_ref, du_ref, dmid_ref, dmb_ref, dn_ref, ds_ref, sum_ref,
     ctx_s, den_s, unit_s, acc_s, back_s) = rest[-15:]
    rows_all, width = x_ref.shape
    seqs, heads = pq_ref.shape[0], pq_ref.shape[1]
    blocks = g_ref.shape[1] // width
    hidden = g_ref.shape[1]

    def attend(s, carry):
        rows = pl.ds(pl.multiple_of(s * PAIR, PAIR), PAIR)
        lane, sub = lanes(), subs()
        zsum = pri_ref[s, width : width + ZROWS, :].astype(F32)
        for p in range(heads // 2):
            at = slice(p * PAIR, (p + 1) * PAIR)
            left, dens = [], []
            for h in (2 * p, 2 * p + 1):
                phi = pq_ref[s, h].T
                score = jnp.where(sub >= lane, dot(phi, pk_ref[s, h]), 0.0).astype(LOW)
                dens.append(
                    jnp.sum(
                        score.astype(F32) + phi.astype(F32) * zsum[h : h + 1, :],
                        axis=1,
                        keepdims=True,
                    )
                )
                left.append(jnp.concatenate([score, phi], axis=1))
            right = jnp.concatenate([v_ref[rows, at], pri_ref[s, at, :]], axis=0)
            both = dot(jnp.concatenate(left, axis=0), right)
            numer = jnp.where(lane < HD, both[:PAIR], both[PAIR:])
            den = jnp.where(lane < HD, dens[0], dens[1])
            ctx = numer / den
            ctx_s[rows, at] = ctx
            den_s[rows, at] = den
            a_ref[rows, at] = ctx.astype(LOW)
        return carry

    lax.fori_loop(0, seqs, attend, 0)

    w_out = w_ref[:, 2 * hidden : 2 * hidden + width]
    mid = x_ref[...].astype(F32) + dot(a_ref[...], w_out) + vec_ref[6:7, :]
    acc_s[...] = mid + vec_ref[12:13, :]
    unit, scale = normed(mid)
    unit_s[...] = unit
    h2_ref[...] = (unit * vec_ref[1:2, :] + vec_ref[7:8, :]).astype(LOW)
    back_s[...] = jnp.zeros_like(back_s)
    c0 = 0.7978845608028654
    c1 = 0.044715

    def mlp(j, carry):
        at = pl.ds(pl.multiple_of(j * width, width), width)
        at2 = pl.ds(pl.multiple_of(hidden + j * width, width), width)
        u = dot(h2_ref[...], w_ref[:, at]) + vec_ref[pl.ds(8 + j, 1), :]
        dg = dot_nt(dy_ref[...], w_ref[:, at2])
        sq = u * u
        th = jnp.tanh(c0 * (u + c1 * (u * sq)))
        half = 0.5 + 0.5 * th
        g = (u * half).astype(LOW)
        slope = half + (0.5 * u) * ((1.0 - th * th) * (c0 + (3.0 * c0 * c1) * sq))
        du = (slope * dg).astype(LOW)
        g_ref[:, at] = g
        du_ref[:, at] = du
        sum_ref[pl.ds(8 + j, 1), :] = jnp.sum(du.astype(F32), axis=0, keepdims=True)
        acc_s[...] += dot(g, w_ref[:, at2])
        back_s[...] += dot_nt(du, w_ref[:, at])
        return carry

    lax.fori_loop(0, blocks, mlp, 0)
    out_ref[...] = acc_s[...].astype(LOW)
    dy = dy_ref[...].astype(F32)
    e = back_s[...]
    unit = unit_s[...]
    sum_ref[12:13, :] = jnp.sum(dy, axis=0, keepdims=True)
    sum_ref[1:2, :] = jnp.sum(e * unit, axis=0, keepdims=True)
    sum_ref[7:8, :] = jnp.sum(e, axis=0, keepdims=True)
    dmid = dy + norm_back(e, vec_ref[1:2, :], unit, scale)
    dmid_ref[...] = dmid
    dmb = dmid.astype(LOW)
    dmb_ref[...] = dmb
    sum_ref[6:7, :] = jnp.sum(dmb.astype(F32), axis=0, keepdims=True)
    back_s[...] = dot_nt(dmb, w_ref[:, 2 * hidden : 2 * hidden + width])

    def back(s, carry):
        rows = pl.ds(pl.multiple_of(s * PAIR, PAIR), PAIR)
        lane = lanes()
        low = lane < HD
        cols = jnp.zeros((PAIR, PAIR), F32)
        for p in range(heads // 2):
            at = slice(p * PAIR, (p + 1) * PAIR)
            dctx = back_s[rows, at]
            inv = 1.0 / den_s[rows, at]
            dn = dctx * inv
            prod = dctx * ctx_s[rows, at]
            swapped = pltpu.roll(inv, HD, 1)
            got = []
            for h, mine, first in ((2 * p, low, HD), (2 * p + 1, jnp.logical_not(low), 0)):
                dd = -jnp.sum(jnp.where(mine, prod, 0.0), axis=1, keepdims=True) * swapped
                rest_dd = dd - dd.astype(LOW).astype(F32)
                tail = jnp.where(lane == first, dd, jnp.where(lane == first + 1, rest_dd, 0.0))
                aug = jnp.where(mine, dn, tail).astype(LOW)
                dn_ref[rows, h * PAIR : (h + 1) * PAIR] = aug
                ds = dot(pq_ref[s, h], aug)
                got.append(ds)
                edge = jnp.logical_or(lane == first, lane == first + 1)
                col = jnp.sum(jnp.where(edge, ds, 0.0), axis=1, keepdims=True)
                cols = jnp.where(lane == h, col, cols)
            ds_ref[s, at, :] = jnp.where(low, got[0], got[1]).astype(LOW)
        ds_ref[s, width : width + ZROWS, :] = cols.T[:ZROWS].astype(LOW)
        return carry

    lax.fori_loop(0, seqs, back, 0)


def leave_kernel(
    x_ref, qkv_ref, pq_ref, pk_ref, pri_ref, dl_ref, dn_ref, dmid_ref, w_ref, maps_ref, vec_ref, *rest
):
    dqkv_ref, dx_ref, gmap_ref, sum_ref = rest[-4:]
    width = x_ref.shape[1]
    seqs, heads = pq_ref.shape[0], pq_ref.shape[1]
    gmap_ref[...] = jnp.zeros_like(gmap_ref)

    def back(s, carry):
        rows = pl.ds(pl.multiple_of(s * PAIR, PAIR), PAIR)
        lane, sub = lanes(), subs()
        low = lane < HD
        fill = jnp.zeros((PAIR - ZROWS, PAIR), F32)
        zcol = jnp.concatenate([pri_ref[s, width : width + ZROWS, :].astype(F32), fill], axis=0).T
        dzcol = jnp.concatenate([dl_ref[s, width : width + ZROWS, :].astype(F32), fill], axis=0).T
        for p in range(heads // 2):
            at = slice(p * PAIR, (p + 1) * PAIR)
            vp = qkv_ref[rows, 2 * width + p * PAIR : 2 * width + (p + 1) * PAIR]
            prior = pri_ref[s, at, :]
            dl = dl_ref[s, at, :]
            left, dfq, dfk, dns = [], [], [], []
            for h, mine, first in ((2 * p, low, HD), (2 * p + 1, jnp.logical_not(low), 0)):
                edge = jnp.logical_or(lane == first, lane == first + 1)
                pq, pk = pq_ref[s, h], pk_ref[s, h]
                dn = dn_ref[rows, h * PAIR : (h + 1) * PAIR]
                vaug = jnp.where(mine, vp.astype(F32), jnp.where(edge, 1.0, 0.0)).astype(LOW)
                saug = jnp.where(
                    mine, prior.astype(F32), jnp.where(edge, zcol[:, h : h + 1], 0.0)
                ).astype(LOW)
                laug = jnp.where(
                    mine, dl.astype(F32), jnp.where(lane == first, dzcol[:, h : h + 1], 0.0)
                ).astype(LOW)
                da = jnp.where(sub >= lane, dot_nt(dn, vaug), 0.0).astype(LOW)
                dpq = dot_nt(
                    jnp.concatenate([pk, saug], axis=1), jnp.concatenate([da, dn], axis=1)
                )
                dpk = dot(pq, da) + dot_nt(laug, vaug)
                dfq.append(soft_back(pq.astype(F32), dpq).astype(LOW))
                dfk.append(soft_back(pk.astype(F32), dpk).astype(LOW))
                keys = pk.T
                score = jnp.where(sub <= lane, dot(keys, pq), 0.0).astype(LOW)
                left.append(jnp.concatenate([score, keys], axis=1))
                dns.append(dn)
            dn = jnp.where(low, dns[0].astype(F32), dns[1].astype(F32)).astype(LOW)
            both = dot(jnp.concatenate(left, axis=0), jnp.concatenate([dn, dl], axis=0))
            dv = jnp.where(low, both[:PAIR], both[PAIR:])
            dqkv_ref[rows, 2 * width + p * PAIR : 2 * width + (p + 1) * PAIR] = dv.astype(LOW)
            for which, parts in ((0, dfq), (1, dfk)):
                df = jnp.concatenate(parts, axis=0)
                mine_at = slice(which * width + p * PAIR, which * width + (p + 1) * PAIR)
                gmap_ref[which, p] += dot(df, qkv_ref[rows, mine_at])
                dqkv_ref[rows, mine_at] = dot(df.T, maps_ref[which, p]).astype(LOW)
        return carry

    lax.fori_loop(0, seqs, back, 0)
    e = dot_nt(dqkv_ref[...], w_ref[...])
    unit, scale = normed(x_ref[...].astype(F32))
    dx_ref[...] = dmid_ref[...] + norm_back(e, vec_ref[0:1, :], unit, scale)
    sum_ref[...] = jnp.zeros_like(sum_ref)
    sum_ref[0:1, :] = jnp.sum(e * unit, axis=0, keepdims=True)
    sum_ref[2:3, :] = jnp.sum(e, axis=0, keepdims=True)
    for part in range(3):
        piece = dqkv_ref[:, part * width : (part + 1) * width].astype(F32)
        sum_ref[3 + part : 4 + part, :] = jnp.sum(piece, axis=0, keepdims=True)


def weight_kernel(h2_ref, du_ref, g_ref, dy_ref, a_ref, dmb_ref, out_ref):
    step = pl.program_id(0)
    blocks = (pl.num_programs(0) - 1) // 2

    @pl.when(step < blocks)
    def _():
        out_ref[...] = dot_tn(h2_ref[...], du_ref[...]).astype(LOW)

    @pl.when(jnp.logical_and(step >= blocks, step < 2 * blocks))
    def _():
        out_ref[...] = dot_tn(g_ref[...], dy_ref[...]).astype(LOW)

    @pl.when(step == 2 * blocks)
    def _():
        out_ref[...] = dot_tn(a_ref[...], dmb_ref[...]).astype(LOW)


def first_kernel(h_ref, d_ref, out_ref):
    out_ref[...] = dot_tn(h_ref[...], d_ref[...]).astype(LOW)


def whole(shape):
    return pl.BlockSpec(shape, lambda i: (0,) * len(shape), pipeline_mode=pl.Buffered(1))


def part(shape, *at):
    return pl.BlockSpec(shape, lambda i: at, pipeline_mode=pl.Buffered(1))


PARAMS = dict(
    compiler_params=pltpu.CompilerParams(
        dimension_semantics=("arbitrary",), vmem_limit_bytes=VMEM_BYTES
    )
)


def cost(flops, size):
    return pl.CostEstimate(flops=int(flops), bytes_accessed=int(size), transcendentals=0)


def enter(m, held, x, w, maps, vec, heads):
    total, width = x.shape
    rows = total // 2
    seqs = rows // PAIR
    pack = width + ZROWS
    return pl.pallas_call(
        enter_kernel,
        grid=(1,),
        in_specs=[
            part((rows, width), m, 0),
            whole(w.shape),
            whole(maps.shape),
            whole(vec.shape),
        ],
        out_specs=[
            whole((rows, width)),
            whole((rows, 3 * width)),
            whole((seqs, heads, PAIR, PAIR)),
            whole((seqs, heads, PAIR, PAIR)),
            whole((seqs, pack, PAIR)),
        ],
        out_shape=[
            jax.ShapeDtypeStruct((rows, width), LOW),
            jax.ShapeDtypeStruct((rows, 3 * width), LOW),
            jax.ShapeDtypeStruct((seqs, heads, PAIR, PAIR), LOW),
            jax.ShapeDtypeStruct((seqs, heads, PAIR, PAIR), LOW),
            jax.ShapeDtypeStruct((seqs, pack, PAIR), LOW),
        ],
        cost_estimate=cost(6 * rows * width * width, 12 * rows * width),
        name="enter",
        **PARAMS,
    )(x, w, maps, vec)


def middle(m, held, x, dy, qkv, pq, pk, pri, w, vec, hidden):
    total, width = x.shape
    rows = total // 2
    seqs, heads = pq.shape[0], pq.shape[1]
    pack = width + ZROWS
    extra = [] if held is None else list(held)
    shared = [
        ((total, width), LOW, (rows, width)),
        ((total, width), LOW, (rows, width)),
        ((total, width), LOW, (rows, width)),
        ((total, hidden), LOW, (rows, hidden)),
        ((total, hidden), LOW, (rows, hidden)),
        ((total, width), F32, (rows, width)),
        ((total, width), LOW, (rows, width)),
    ]
    return pl.pallas_call(
        middle_kernel,
        grid=(1,),
        in_specs=[
            part((rows, width), m, 0),
            part((rows, width), m, 0),
            part((rows, width), 0, 2),
            whole(pq.shape),
            whole(pk.shape),
            whole(pri.shape),
            whole(w.shape),
            whole(vec.shape),
        ]
        + [pl.BlockSpec(memory_space=pl.ANY)] * len(extra),
        out_specs=[part(b, m, 0) for _, _, b in shared]
        + [whole((rows, heads * PAIR)), whole((seqs, pack, PAIR)), whole((ZROWS, width))],
        out_shape=[jax.ShapeDtypeStruct(s, t) for s, t, _ in shared]
        + [
            jax.ShapeDtypeStruct((rows, heads * PAIR), LOW),
            jax.ShapeDtypeStruct((seqs, pack, PAIR), LOW),
            jax.ShapeDtypeStruct((ZROWS, width), F32),
        ],
        scratch_shapes=[pltpu.VMEM((rows, width), F32)] * 5,
        input_output_aliases={8 + k: k for k in range(len(extra))},
        cost_estimate=cost(8 * rows * width * hidden + 4 * rows * width * width, 30 * rows * width),
        name="middle",
        **PARAMS,
    )(x, dy, qkv, pq, pk, pri, w, vec, *extra)


def leave(m, held, x, qkv, pq, pk, pri, dl, dn, dmid, w, maps, vec):
    total, width = x.shape
    rows = total // 2
    extra = [] if held is None else list(held)
    return pl.pallas_call(
        leave_kernel,
        grid=(1,),
        in_specs=[
            part((rows, width), m, 0),
            whole(qkv.shape),
            whole(pq.shape),
            whole(pk.shape),
            whole(pri.shape),
            whole(dl.shape),
            whole(dn.shape),
            part((rows, width), m, 0),
            whole(w.shape),
            whole(maps.shape),
            whole(vec.shape),
        ]
        + [pl.BlockSpec(memory_space=pl.ANY)] * len(extra),
        out_specs=[
            part((rows, 3 * width), m, 0),
            part((rows, width), m, 0),
            whole(maps.shape),
            whole((ZROWS, width)),
        ],
        out_shape=[
            jax.ShapeDtypeStruct((total, 3 * width), LOW),
            jax.ShapeDtypeStruct((total, width), F32),
            jax.ShapeDtypeStruct(maps.shape, F32),
            jax.ShapeDtypeStruct((ZROWS, width), F32),
        ],
        input_output_aliases={11 + k: k for k in range(len(extra))},
        cost_estimate=cost(6 * rows * width * width, 24 * rows * width),
        name="leave",
        **PARAMS,
    )(x, qkv, pq, pk, pri, dl, dn, dmid, w, maps, vec, *extra)


def weight_grads(h2, du, g, dy, a, dmb):
    total, width = h2.shape
    blocks = du.shape[1] // width
    last = 2 * blocks
    block = (total, width)
    return pl.pallas_call(
        weight_kernel,
        grid=(last + 1,),
        in_specs=[
            pl.BlockSpec(block, lambda i: (0, 0)),
            pl.BlockSpec(block, lambda i: (0, jnp.minimum(i, blocks - 1))),
            pl.BlockSpec(block, lambda i: (0, jnp.clip(i - blocks, 0, blocks - 1))),
            pl.BlockSpec(block, lambda i: (0, 0)),
            pl.BlockSpec(block, lambda i: (0, 0)),
            pl.BlockSpec(block, lambda i: (0, 0)),
        ],
        out_specs=pl.BlockSpec((width, width), lambda i: (0, i)),
        out_shape=jax.ShapeDtypeStruct((width, (last + 1) * width), LOW),
        cost_estimate=cost(2 * total * width * width * (last + 1), 20 * total * width),
        name="weights",
        **PARAMS,
    )(h2, du, g, dy, a, dmb)


def first_grads(hid, dqkv):
    total, width = hid.shape
    block = (total, width)
    return pl.pallas_call(
        first_kernel,
        grid=(3,),
        in_specs=[pl.BlockSpec(block, lambda i: (0, 0)), pl.BlockSpec(block, lambda i: (0, i))],
        out_specs=pl.BlockSpec((width, width), lambda i: (0, i)),
        out_shape=jax.ShapeDtypeStruct((width, 3 * width), LOW),
        cost_estimate=cost(6 * total * width * width, 12 * total * width),
        name="first",
        **PARAMS,
    )(hid, dqkv)


def shards(tokens, w_qkv, w_feat, w_out, w_fc, w_proj, gains, biases, cotangent):
    micro_count, seq_count, seg_len, width = tokens.shape
    grid = grid_dims()
    rows = w_qkv.shape[0]
    hidden = w_fc.shape[1]
    ratio = hidden // width
    heads = width // HD
    pairs = heads // 2
    wide = 3 * width
    total = micro_count * seq_count * seg_len

    first = jnp.concatenate(
        [
            w_qkv.astype(LOW),
            jnp.transpose(w_feat, (1, 0, 2)).reshape(rows, PAIR).astype(LOW),
            jnp.pad(jnp.concatenate([gains, biases]).T.astype(LOW), ((0, 0), (0, PAIR - 13))),
        ],
        axis=1,
    )
    first = gather_rows(first, grid, ("z", "x", "y", "c"))
    later = jnp.concatenate(
        [
            w_fc.astype(LOW).reshape(rows, width, ratio).swapaxes(1, 2).reshape(rows, hidden),
            w_proj.astype(LOW).reshape(rows, hidden),
            w_out.astype(LOW),
        ],
        axis=1,
    )
    later = lax.all_gather(later, AXES, axis=0, tiled=True)
    small = first[:, wide + PAIR :].T[:13].astype(F32)
    fc_bias = small[8 : 8 + ratio].reshape(width, ratio).T
    vec = jnp.concatenate([small[:8], fc_bias, small[8 + ratio :], jnp.zeros((3, width), F32)])
    maps = first[:, wide : wide + PAIR].reshape(pairs, 2, HD, 2, HD)
    maps = jnp.transpose(maps, (3, 0, 1, 4, 2))
    none = jnp.zeros_like(maps[:, :, 0])
    maps = jnp.concatenate(
        [
            jnp.concatenate([maps[:, :, 0], none], axis=-1),
            jnp.concatenate([none, maps[:, :, 1]], axis=-1),
        ],
        axis=-2,
    )
    w_first = first[:, :wide]
    x = tokens.reshape(total, width)
    dy = cotangent.reshape(total, width)

    entered = [enter(m, None, x, w_first, maps, vec, heads) for m in range(2)]
    priors = [prefix(entered[m][4], grid, False) for m in range(2)]
    held, mids = None, []
    for m in range(2):
        _, qkv, pq, pk, _ = entered[m]
        got = middle(m, held, x, dy, qkv, pq, pk, priors[m], later, vec, hidden)
        held = got[:7]
        mids.append(got[7:])
    out, a, h2, g, du, dmid, dmb = held
    laters = [prefix(mids[m][1], grid, True) for m in range(2)]
    g_later = weight_grads(h2, du, g, dy, a, dmb)
    kept, ends = None, []
    for m in range(2):
        _, qkv, pq, pk, _ = entered[m]
        got = leave(m, kept, x, qkv, pq, pk, priors[m], laters[m], mids[m][0], dmid, w_first, maps, vec)
        kept = got[:2]
        ends.append(got[2:])
    dqkv, dx = kept
    hid = jnp.concatenate([entered[0][0], entered[1][0]])
    g_qkv = first_grads(hid, dqkv)

    gmap = (ends[0][0] + ends[1][0]).reshape(2, pairs, 2, HD, 2, HD)
    gmap = jnp.stack([gmap[:, :, 0, :, 0], gmap[:, :, 1, :, 1]], axis=2)
    gmap = jnp.transpose(gmap, (1, 2, 4, 0, 3)).reshape(width, PAIR)
    inner = mids[0][2] + mids[1][2]
    outer = ends[0][1] + ends[1][1]
    g_fc_bias = inner[8 : 8 + ratio].T.reshape(ratio, width)
    vec_rows = [outer[0:1], inner[1:2], outer[2:6], inner[6:8], g_fc_bias, inner[12:13]]
    g_small = jnp.concatenate(vec_rows).T

    r_fc = scatter_rows(g_later[:, :hidden], grid, ("c", "x", "y", "z"))
    r_proj = scatter_rows(g_later[:, hidden : 2 * hidden], grid, ("c", "y", "x", "z"))
    last = jnp.concatenate(
        [
            g_qkv,
            g_later[:, 2 * hidden :],
            gmap.astype(LOW),
            jnp.pad(g_small.astype(LOW), ((0, 0), (0, PAIR - 13))),
        ],
        axis=1,
    )
    last = scatter_rows(last, grid, ("c", "x", "y", "z")).astype(F32)
    small = last[:, wide + width + PAIR :].T
    return (
        out.reshape(tokens.shape),
        dx.reshape(tokens.shape),
        last[:, :wide],
        jnp.transpose(last[:, wide + width : wide + width + PAIR].reshape(rows, 2, HD), (1, 0, 2)),
        last[:, wide : wide + width],
        r_fc.astype(F32).reshape(rows, ratio, width).swapaxes(1, 2).reshape(rows, hidden),
        r_proj.astype(F32).reshape(rows * ratio, width),
        small[:2],
        small[2:13],
    )


def solution(mesh):
    return jax.shard_map(
        shards,
        mesh=mesh,
        in_specs=(
            P(None, "dp", "seq", None),
            P(("dp", "seq"), None),
            P(None, ("dp", "seq"), None),
            P(("dp", "seq"), None),
            P(("dp", "seq"), None),
            P(("dp", "seq"), None),
            P(None, ("dp", "seq")),
            P(None, ("dp", "seq")),
            P(None, "dp", "seq", None),
        ),
        out_specs=(
            P(None, "dp", "seq", None),
            P(None, "dp", "seq", None),
            P(("dp", "seq"), None),
            P(None, ("dp", "seq"), None),
            P(("dp", "seq"), None),
            P(("dp", "seq"), None),
            P(("dp", "seq"), None),
            P(None, ("dp", "seq")),
            P(None, ("dp", "seq")),
        ),
        check_vma=False,
    )
```

time: 935 us -> 560 us (0.60)
  local copies, waits for them, and re-layouts: 218 us -> 35.5 us
  matrix products: 170 us -> 0 us
  Pallas kernels: 0 us -> 168 us
  other arithmetic: 111 us -> 38.5 us
  waiting for transfers between devices: 306 us -> 235 us
  starting transfers between devices: 107 us -> 57.8 us
    ppermute x40 -> x32, waiting for transfers between devices: 306 us -> 125 us  [send(): return lax.ppermute(value, AXES, turned(sizes, name, step))]
    pallas_call x0 -> x8, Pallas kernels: none -> 168 us  [the longest x2 69.4 us: middle(): pl.pallas_call(middle_kernel, grid=(1,), in_specs=[part((rows, width), m,...]
    dot_general x30 -> x0, matrix products: 157 us -> none  [the longest x4 37.9 us: dot_second(): lax.dot_general(first_op, second_op, (((1,), (1,)), ((), ())), preferred_...]
    ppermute x0 -> x12, waiting for transfers between devices: none -> 110 us  [prefix(): lax.ppermute(mine, AXES, moved(sizes, 'z', sign * k)).astype(F32)]
    ppermute x40 -> x32, starting transfers between devices: 107 us -> 30.6 us  [send(): return lax.ppermute(value, AXES, turned(sizes, name, step))]
    concatenate x12 -> x3, local copies, waits for them, and re-layouts: 66.6 us -> 1.68 us  [the longest x2 1.6 us: shards(): g_small = jnp.concatenate(vec_rows).T]
    unnamed x260 -> x59, local copies, waits for them, and re-layouts: 42.6 us -> 8.25 us
    reduce_sum x15 -> x0, other arithmetic: 33.9 us -> none  [the longest x2 6.79 us: features(): jax.nn.softmax(logits, axis=-1)]
  transfers between devices with their start and end apart: 41 -> 45, of which waited for: 15 -> 21; matrix products, arithmetic and copies ran while one was open for 38% -> 12% of each run, Pallas kernels for 0% -> 24%
where the time goes in v2:
time: 560 us; the launch traced here: 551 us
  waiting for transfers between devices  235 us (42%)
  Pallas kernels  168 us (30%)
  starting transfers between devices  57.8 us (10%)
  other arithmetic  38.5 us (7%)
  local copies, waits for them, and re-layouts  35.5 us (6%)
  between operations  15.5 us (3%)
    ppermute x32, waiting for transfers between devices, send(): return lax.ppermute(value, AXES, turned(sizes, name, step))  125 us
    ppermute x12, waiting for transfers between devices, prefix(): lax.ppermute(mine, AXES, moved(sizes, 'z', sign * k)).astype(F32)  110 us
    pallas_call x2, Pallas kernels, middle(): pl.pallas_call(middle_kernel, grid=(1,), in_specs=[part((rows, width), m,...  69.4 us
    pallas_call x2, Pallas kernels, leave(): pl.pallas_call(leave_kernel, grid=(1,), in_specs=[part((rows, width), m,...  47.3 us
    ppermute x32, starting transfers between devices, send(): return lax.ppermute(value, AXES, turned(sizes, name, step))  30.6 us
    ppermute x12, starting transfers between devices, prefix(): lax.ppermute(mine, AXES, moved(sizes, 'z', sign * k)).astype(F32)  27.1 us
    pallas_call x2, Pallas kernels, enter(): pl.pallas_call(enter_kernel, grid=(1,), in_specs=[part((rows, width), m,...  24.7 us
    pallas_call x1, Pallas kernels, weight_grads(): pl.pallas_call(weight_kernel, grid=(last + 1,), in_specs=[pl.BlockSpec(bl...  19.3 us
  transfers between devices with their start and end apart: 45, of which 21 were waited for; matrix products, arithmetic and copies ran while one was open for 12% of the time, Pallas kernels for 24%

profile of v2, /device:TPU:0, one launch (start us, length us, event | category | flops | bytes accessed | tf_op | source)
XLA Modules:
  0.0 550.9 jit_solution(14624178618762570499)
XLA Ops:
  10.6 5.1 collective-permute-start
  19.4 7.0 %collective-permute-done.1 = bf16[24,2560]{1,0:T(8,128)(2,1)S(1)} collective-permute-done((bf16[24,2560]{1,0:T(8,128)(2,1)S(1)}, bf16[24,2560]{1,0:T(8,128)(2,1)S(1)}, u32[]{:S(2)}, u32[]{:S(2)}) %collective-permute-start.1) | collective-permute-done | bytes 122912 | tf_op jit(solution)/shard_map/ppermute | solution.py:46
  28.1 10.9 %collective-permute-done.3 = bf16[4,24,2560]{2,1,0:T(8,128)(2,1)S(1)} collective-permute-done((bf16[4,24,2560]{2,1,0:T(8,128)(2,1)S(1)}, bf16[4,24,2560]{2,1,0:T(8,128)(2,1)S(1)}, u32[]{:S(2)}, u32[]{:S(2)}) %collective-permute-start.3) | collective-permute-done | bytes 491552 | tf_op jit(solution)/shard_map/ppermute | solution.py:46
  40.7 25.4 %collective-permute-done.4 = bf16[2,4,24,2560]{3,2,1,0:T(8,128)(2,1)} collective-permute-done((bf16[2,4,24,2560]{3,2,1,0:T(8,128)(2,1)S(1)}, bf16[2,4,24,2560]{3,2,1,0:T(8,128)(2,1)}, u32[]{:S(2)}, u32[]{:S(2)}) %collective-permute-start.4) | collective-permute-done | bytes 983072 | tf_op jit(solution)/shard_map/ppermute | solution.py:46
  69.0 4.7 collective-permute-done.5
  84.9 12.3 %enter.3 = (bf16[512,768]{1,0:T(8,128)(2,1)}, bf16[512,2304]{1,0:T(8,128)(2,1)}, bf16[4,12,128,128]{3,2,1,0:T(8,128)(2,1)}, bf16[4,12,128,128]{3,2,1,0:T(8,128)(2,1)}, bf16[4,784,128]{2,1,0:T(8,128)(2,1)}) custom-call(bf16[1024,768]{1,0:T(8,128)(2,1)} %bitcast.152, bf16[768,2304]{1,0:T(8,128)(2,1)} %slice.112.w_ref, ...), custom_call_target="tpu_custom_call" | custom-call | flops 1811939328 | bytes 4718592 | tf_op jit(solution)/shard_map/enter/pallas_call | solution.py:436
  97.4 12.4 %enter.2 = (bf16[512,768]{1,0:T(8,128)(2,1)}, bf16[512,2304]{1,0:T(8,128)(2,1)}, bf16[4,12,128,128]{3,2,1,0:T(8,128)(2,1)}, bf16[4,12,128,128]{3,2,1,0:T(8,128)(2,1)}, bf16[4,784,128]{2,1,0:T(8,128)(2,1)}) custom-call(bf16[1024,768]{1,0:T(8,128)(2,1)} %bitcast.153, bf16[768,2304]{1,0:T(8,128)(2,1)} %slice.112.w_ref, ...), custom_call_target="tpu_custom_call" | custom-call | flops 1811939328 | bytes 4718592 | tf_op jit(solution)/shard_map/enter/pallas_call | solution.py:436
  133.3 8.6 %collective-permute-done.14 = bf16[2,784,128]{2,1,0:T(8,128)(2,1)} collective-permute-done((bf16[2,784,128]{2,1,0:T(8,128)(2,1)}, bf16[2,784,128]{2,1,0:T(8,128)(2,1)}, u32[]{:S(2)}, u32[]{:S(2)}) %collective-permute-start.14) | collective-permute-done | bytes 401440 | tf_op jit(solution)/shard_map/ppermute | solution.py:118
  143.4 7.1 %collective-permute-done.7 = bf16[2,784,128]{2,1,0:T(8,128)(2,1)} collective-permute-done((bf16[2,784,128]{2,1,0:T(8,128)(2,1)}, bf16[2,784,128]{2,1,0:T(8,128)(2,1)}, u32[]{:S(2)}, u32[]{:S(2)}) %collective-permute-start.7) | collective-permute-done | bytes 401440 | tf_op jit(solution)/shard_map/ppermute | solution.py:118
  150.5 8.6 %collective-permute-done.8 = bf16[2,784,128]{2,1,0:T(8,128)(2,1)} collective-permute-done((bf16[2,784,128]{2,1,0:T(8,128)(2,1)}, bf16[2,784,128]{2,1,0:T(8,128)(2,1)}, u32[]{:S(2)}, u32[]{:S(2)}) %collective-permute-start.8) | collective-permute-done | bytes 401440 | tf_op jit(solution)/shard_map/ppermute | solution.py:118
  159.2 8.2 %collective-permute-done.9 = bf16[2,784,128]{2,1,0:T(8,128)(2,1)} collective-permute-done((bf16[2,784,128]{2,1,0:T(8,128)(2,1)}, bf16[2,784,128]{2,1,0:T(8,128)(2,1)}, u32[]{:S(2)}, u32[]{:S(2)}) %collective-permute-start.9) | collective-permute-done | bytes 401440 | tf_op jit(solution)/shard_map/ppermute | solution.py:118
  173.0 34.6 %middle.2 = (bf16[1024,768]{1,0:T(8,128)(2,1)}, bf16[1024,768]{1,0:T(8,128)(2,1)}, bf16[1024,768]{1,0:T(8,128)(2,1)}, bf16[1024,3072]{1,0:T(8,128)(2,1)}, bf16[1...) custom-call(bf16[1024,768]{1,0:T(8,128)(2,1)} %bitcast.154, ...), custom_call_target="tpu_custom_call" | custom-call | flops 10871635968 | bytes 11796480 | tf_op jit(solution)/shard_map/middle/pallas_call | solution.py:480
  207.7 34.8 %middle.3 = (bf16[1024,768]{1,0:T(8,128)(2,1)}, bf16[1024,768]{1,0:T(8,128)(2,1)}, bf16[1024,768]{1,0:T(8,128)(2,1)}, bf16[1024,3072]{1,0:T(8,128)(2,1)}, bf16[1...) custom-call(bf16[1024,768]{1,0:T(8,128)(2,1)} %bitcast.155, ...), custom_call_target="tpu_custom_call", output_to_operand_aliasing={{0}: (8, {}), {1}: (9, {}), {2}: (10, {}), {3}: (11, {}), {... | custom-call | flops 10871635968 | bytes 11796480 | tf_op jit(solution)/shard_map/middle/pallas_call | solution.py:480
  242.5 19.3 %weights.1 = bf16[768,6912]{1,0:T(8,128)(2,1)} custom-call(bf16[1024,768]{1,0:T(8,128)(2,1)} %get-tuple-element.74.h2_ref, bf16[1024,3072]{1,0:T(8,128)(2,1)} %get-tuple-element.75.du_ref, bf16[1024,3072]{1,0:T(8,128)(2,1)} %get-tuple-element.76.g_ref, bf16[1024,768]{1,0:T(8,128)(2,1)} %bitcast.164, bf16[1024,768]{1,0:T(8,128)(2,1)} %get-tuple-element.77.a_ref, ...), custom_call_target="tpu_custom_call" | custom-call | flops 10871635968 | bytes 15728640 | tf_op jit(solution)/shard_map/weights/pallas_call | solution.py:555
  282.1 19.1 %collective-permute-done.22 = bf16[2,784,128]{2,1,0:T(8,128)(2,1)S(1)} collective-permute-done((bf16[2,784,128]{2,1,0:T(8,128)(2,1)S(1)}, bf16[2,784,128]{2,1,0:T(8,128)(2,1)S(1)}, u32[]{:S(2)}, u32[]{:S(2)}) %collective-permute-start.22) | collective-permute-done | bytes 401440 | tf_op jit(solution)/shard_map/ppermute | solution.py:118
  303.0 26.2 %collective-permute-done.23 = bf16[2,784,128]{2,1,0:T(8,128)(2,1)S(1)} collective-permute-done((bf16[2,784,128]{2,1,0:T(8,128)(2,1)S(1)}, bf16[2,784,128]{2,1,0:T(8,128)(2,1)S(1)}, u32[]{:S(2)}, u32[]{:S(2)}) %collective-permute-start.23) | collective-permute-done | bytes 401440 | tf_op jit(solution)/shard_map/ppermute | solution.py:118
  331.7 31.0 %collective-permute-done.18 = bf16[2,784,128]{2,1,0:T(8,128)(2,1)} collective-permute-done((bf16[2,784,128]{2,1,0:T(8,128)(2,1)}, bf16[2,784,128]{2,1,0:T(8,128)(2,1)}, u32[]{:S(2)}, u32[]{:S(2)}) %collective-permute-start.18) | collective-permute-done | bytes 401440 | tf_op jit(solution)/shard_map/ppermute | solution.py:118
  369.5 23.7 %leave.2 = (bf16[1024,2304]{1,0:T(8,128)(2,1)}, f32[1024,768]{1,0:T(8,128)}, f32[2,6,128,128]{3,2,1,0:T(8,128)}, f32[16,768]{1,0:T(8,128)}) custom-call(bf16[1024,768]{1,0:T(8,128)(2,1)} %bitcast.156, bf16[512,2304]{1,0:T(8,128)(2,1)} %get-tuple-element.51.v_ref.qkv_ref, bf16[4,12,128,128]{3,2,1,0:T(8,128)(2,1)} %get-tuple-element.52.pq_ref, ...), custom_call_target="tpu_custom_call" | custom-call | flops 1811939328 | bytes 9437184 | tf_op jit(solution)/shard_map/leave/pallas_call | solution.py:514
  393.2 23.6 %leave.3 = (bf16[1024,2304]{1,0:T(8,128)(2,1)}, f32[1024,768]{1,0:T(8,128)}, f32[2,6,128,128]{3,2,1,0:T(8,128)}, f32[16,768]{1,0:T(8,128)}) custom-call(bf16[1024,768]{1,0:T(8,128)(2,1)} %bitcast.157, bf16[512,2304]{1,0:T(8,128)(2,1)} %get-tuple-element.47.v_ref.qkv_ref, ...), custom_call_target="tpu_custom_call", output_to_operand_aliasing={{0}: (11, {}), {1}: (12, {})} | custom-call | flops 1811939328 | bytes 9437184 | tf_op jit(solution)/shard_map/leave/pallas_call | solution.py:514
  425.7 7.8 %first.1 = bf16[768,2304]{1,0:T(8,128)(2,1)} custom-call(bf16[1024,768]{1,0:T(8,128)(2,1)} %pad_maximum_fusion.2.h_ref, bf16[1024,2304]{1,0:T(8,128)(2,1)} %get-tuple-element.73.d_ref), custom_call_target="tpu_custom_call" | custom-call | flops 3623878656 | bytes 9437184 | tf_op jit(solution)/shard_map/first/pallas_call | solution.py:577
  444.2 23.8 %collective-permute-done.39 = bf16[2,4,24,3072]{3,2,1,0:T(8,128)(2,1)S(1)} collective-permute-done((bf16[2,4,24,3072]{3,2,1,0:T(8,128)(2,1)S(1)}, bf16[2,4,24,3072]{3,2,1,0:T(8,128)(2,1)S(1)}, u32[]{:S(2)}, u32[]{:S(2)}) %collective-permute-start.39) | collective-permute-done | bytes 1179680 | tf_op jit(solution)/shard_map/ppermute | solution.py:46
  472.5 10.6 %collective-permute-done.40 = bf16[4,24,3072]{2,1,0:T(8,128)(2,1)S(1)} collective-permute-done((bf16[4,24,3072]{2,1,0:T(8,128)(2,1)S(1)}, bf16[4,24,3072]{2,1,0:T(8,128)(2,1)S(1)}, u32[]{:S(2)}, u32[]{:S(2)}) %collective-permute-start.40) | collective-permute-done | bytes 589856 | tf_op jit(solution)/shard_map/ppermute | solution.py:46
  490.3 22.3 %collective-permute-done.27 = bf16[2,4,24,3328]{3,2,1,0:T(8,128)(2,1)S(1)} collective-permute-done((bf16[2,4,24,3328]{3,2,1,0:T(8,128)(2,1)S(1)}, bf16[2,4,24,3328]{3,2,1,0:T(8,128)(2,1)S(1)}, u32[]{:S(2)}, u32[]{:S(2)}) %collective-permute-start.27) | collective-permute-done | bytes 1277984 | tf_op jit(solution)/shard_map/ppermute | solution.py:46
  514.8 12.3 %collective-permute-done.28 = bf16[4,24,3328]{2,1,0:T(8,128)(2,1)S(1)} collective-permute-done((bf16[4,24,3328]{2,1,0:T(8,128)(2,1)S(1)}, bf16[4,24,3328]{2,1,0:T(8,128)(2,1)S(1)}, u32[]{:S(2)}, u32[]{:S(2)}) %collective-permute-start.28) | collective-permute-done | bytes 639008 | tf_op jit(solution)/shard_map/ppermute | solution.py:46
  (245 shorter events, 135.8 us)
Async XLA Ops:
  7.2 165.7 %all-gather.2.cloned.1.call-start = ((), (), s32[]{:S(2)}) async-start(), calls=%async_computation | async-start | bytes 10948608 | tf_op jit(solution)/shard_map/all_gather | solution.py:617
  39.1 27.0 %collective-permute-start.4 = (bf16[2,4,24,2560]{3,2,1,0:T(8,128)(2,1)S(1)}, bf16[2,4,24,2560]{3,2,1,0:T(8,128)(2,1)}, u32[]{:S(2)}, u32[]{:S(2)}) collective-permute-start(bf16[2,4,24,2560]{3,2,1,0:T(8,128)(2,1)S(1)} %pad_maximum_fusion.3), channel_id=1, source_target_pairs={{0,16},{1,17},{2,18},{3,19},{4,20},{5,21},{6,22},{7,23},{8,24},{9,... | collective-permute-start | bytes 2949128 | tf_op jit(solution)/shard_map/ppermute | solution.py:46
  124.0 26.6 %collective-permute-start.7 = (bf16[2,784,128]{2,1,0:T(8,128)(2,1)}, bf16[2,784,128]{2,1,0:T(8,128)(2,1)}, u32[]{:S(2)}, u32[]{:S(2)}) collective-permute-start(bf16[2,784,128]{2,1,0:T(8,128)(2,1)} %add_convert_fusion.11), channel_id=1, source_target_pairs={{0,2},{1,3},{2,4},{3,5},{4,6},{5,7},{8,10},{9,11},{10,12},{11,13},... | collective-permute-start | bytes 1204232 | tf_op jit(solution)/shard_map/ppermute | solution.py:118
  126.0 33.2 %collective-permute-start.8 = (bf16[2,784,128]{2,1,0:T(8,128)(2,1)}, bf16[2,784,128]{2,1,0:T(8,128)(2,1)}, u32[]{:S(2)}, u32[]{:S(2)}) collective-permute-start(bf16[2,784,128]{2,1,0:T(8,128)(2,1)} %add_convert_fusion.11), channel_id=1, source_target_pairs={{0,4},{1,5},{2,6},{3,7},{8,12},{9,13},{10,14},{11,15},{16,20},{17,... | collective-permute-start | bytes 1204232 | tf_op jit(solution)/shard_map/ppermute | solution.py:118
  128.0 39.3 %collective-permute-start.9 = (bf16[2,784,128]{2,1,0:T(8,128)(2,1)}, bf16[2,784,128]{2,1,0:T(8,128)(2,1)}, u32[]{:S(2)}, u32[]{:S(2)}) collective-permute-start(bf16[2,784,128]{2,1,0:T(8,128)(2,1)} %add_convert_fusion.11), channel_id=1, source_target_pairs={{0,6},{1,7},{8,14},{9,15},{16,22},{17,23},{24,30},{25,31}} | collective-permute-start | bytes 1204232 | tf_op jit(solution)/shard_map/ppermute | solution.py:118
  143.3 26.8 %collective-permute-start.15 = (bf16[2,784,128]{2,1,0:T(8,128)(2,1)S(1)}, bf16[2,784,128]{2,1,0:T(8,128)(2,1)S(1)}, u32[]{:S(2)}, u32[]{:S(2)}) collective-permute-start(bf16[2,784,128]{2,1,0:T(8,128)(2,1)S(1)} %add_convert_fusion.8), channel_id=1, source_target_pairs={{0,1},{1,0},{2,3},{3,2},{4,5},{5,4},{6,7},{7,6},{8,9},{9,8},{10,11... | collective-permute-start | bytes 1204232 | tf_op jit(solution)/shard_map/ppermute | solution.py:46
  207.5 61.1 %collective-permute-start.21 = (bf16[4,784,128]{2,1,0:T(8,128)(2,1)}, bf16[4,784,128]{2,1,0:T(8,128)(2,1)}, u32[]{:S(2)}, u32[]{:S(2)}) collective-permute-start(bf16[4,784,128]{2,1,0:T(8,128)(2,1)} %get-tuple-element.66), channel_id=1, source_target_pairs={{0,1},{1,0},{2,3},{3,2},{4,5},{5,4},{6,7},{7,6},{8,9},{9,8},{10,11... | collective-permute-start | bytes 2408456 | tf_op jit(solution)/shard_map/ppermute | solution.py:46
  270.0 31.2 %collective-permute-start.22 = (bf16[2,784,128]{2,1,0:T(8,128)(2,1)S(1)}, bf16[2,784,128]{2,1,0:T(8,128)(2,1)S(1)}, u32[]{:S(2)}, u32[]{:S(2)}) collective-permute-start(bf16[2,784,128]{2,1,0:T(8,128)(2,1)S(1)} %add_convert_fusion.5), channel_id=1, source_target_pairs={{2,0},{3,1},{4,2},{5,3},{6,4},{7,5},{10,8},{11,9},{12,10},{13,11},... | collective-permute-start | bytes 1204232 | tf_op jit(solution)/shard_map/ppermute | solution.py:118
  273.0 56.2 %collective-permute-start.23 = (bf16[2,784,128]{2,1,0:T(8,128)(2,1)S(1)}, bf16[2,784,128]{2,1,0:T(8,128)(2,1)S(1)}, u32[]{:S(2)}, u32[]{:S(2)}) collective-permute-start(bf16[2,784,128]{2,1,0:T(8,128)(2,1)S(1)} %add_convert_fusion.5), channel_id=1, source_target_pairs={{4,0},{5,1},{6,2},{7,3},{12,8},{13,9},{14,10},{15,11},{20,16},{21,... | collective-permute-start | bytes 1204232 | tf_op jit(solution)/shard_map/ppermute | solution.py:118
  274.3 54.9 %collective-permute-start.24 = (bf16[2,784,128]{2,1,0:T(8,128)(2,1)S(1)}, bf16[2,784,128]{2,1,0:T(8,128)(2,1)S(1)}, u32[]{:S(2)}, u32[]{:S(2)}) collective-permute-start(bf16[2,784,128]{2,1,0:T(8,128)(2,1)S(1)} %add_convert_fusion.5), channel_id=1, source_target_pairs={{6,0},{7,1},{14,8},{15,9},{22,16},{23,17},{30,24},{31,25}} | collective-permute-start | bytes 1204232 | tf_op jit(solution)/shard_map/ppermute | solution.py:118
  279.5 52.1 %collective-permute-start.17 = (bf16[2,784,128]{2,1,0:T(8,128)(2,1)}, bf16[2,784,128]{2,1,0:T(8,128)(2,1)}, u32[]{:S(2)}, u32[]{:S(2)}) collective-permute-start(bf16[2,784,128]{2,1,0:T(8,128)(2,1)} %add_convert_fusion.7), channel_id=1, source_target_pairs={{2,0},{3,1},{4,2},{5,3},{6,4},{7,5},{10,8},{11,9},{12,10},{13,11},... | collective-permute-start | bytes 1204232 | tf_op jit(solution)/shard_map/ppermute | solution.py:118
  280.8 81.9 %collective-permute-start.18 = (bf16[2,784,128]{2,1,0:T(8,128)(2,1)}, bf16[2,784,128]{2,1,0:T(8,128)(2,1)}, u32[]{:S(2)}, u32[]{:S(2)}) collective-permute-start(bf16[2,784,128]{2,1,0:T(8,128)(2,1)} %add_convert_fusion.7), channel_id=1, source_target_pairs={{4,0},{5,1},{6,2},{7,3},{12,8},{13,9},{14,10},{15,11},{20,16},{21,... | collective-permute-start | bytes 1204232 | tf_op jit(solution)/shard_map/ppermute | solution.py:118
  301.2 61.5 %collective-permute-start.19 = (bf16[2,784,128]{2,1,0:T(8,128)(2,1)}, bf16[2,784,128]{2,1,0:T(8,128)(2,1)}, u32[]{:S(2)}, u32[]{:S(2)}) collective-permute-start(bf16[2,784,128]{2,1,0:T(8,128)(2,1)} %add_convert_fusion.7), channel_id=1, source_target_pairs={{6,0},{7,1},{14,8},{15,9},{22,16},{23,17},{30,24},{31,25}} | collective-permute-start | bytes 1204232 | tf_op jit(solution)/shard_map/ppermute | solution.py:118
  329.2 107.2 %collective-permute-start.38 = (bf16[2,2,4,24,3072]{4,3,2,1,0:T(8,128)(2,1)}, bf16[2,2,4,24,3072]{4,3,2,1,0:T(8,128)(2,1)}, u32[]{:S(2)}, u32[]{:S(2)}) collective-permute-start(bf16[2,2,4,24,3072]{4,3,2,1,0:T(8,128)(2,1)} %dynamic-slice_bitcast_fusion.1), channel_id=1, source_target_pairs={{0,1},{1,0},{2,3},{3,2},{4,5},{5,4},{6,7},{7,6},{8,9},{9,8},{10,11... | collective-permute-start | bytes 7077896 | tf_op jit(solution)/shard_map/ppermute | solution.py:46
  329.9 111.4 %collective-permute-start.32 = (bf16[2,2,4,24,3072]{4,3,2,0,1:T(8,128)(2,1)}, bf16[2,2,4,24,3072]{4,3,2,0,1:T(8,128)(2,1)S(1)}, u32[]{:S(2)}, u32[]{:S(2)}) collective-permute-start(bf16[2,2,4,24,3072]{4,3,2,0,1:T(8,128)(2,1)} %bitcast.161), channel_id=1, source_target_pairs={{0,1},{1,0},{2,3},{3,2},{4,5},{5,4},{6,7},{7,6},{8,9},{9,8},{10,11... | collective-permute-start | bytes 7077896 | tf_op jit(solution)/shard_map/ppermute | solution.py:46
  331.6 33.9 %collective-permute-start.25 = (bf16[2,784,128]{2,1,0:T(8,128)(2,1)S(1)}, bf16[2,784,128]{2,1,0:T(8,128)(2,1)S(1)}, u32[]{:S(2)}, u32[]{:S(2)}) collective-permute-start(bf16[2,784,128]{2,1,0:T(8,128)(2,1)S(1)} %add_convert_fusion.4), channel_id=1, source_target_pairs={{0,1},{1,0},{2,3},{3,2},{4,5},{5,4},{6,7},{7,6},{8,9},{9,8},{10,11... | collective-permute-start | bytes 1204232 | tf_op jit(solution)/shard_map/ppermute | solution.py:46
  439.8 28.2 %collective-permute-start.39 = (bf16[2,4,24,3072]{3,2,1,0:T(8,128)(2,1)S(1)}, bf16[2,4,24,3072]{3,2,1,0:T(8,128)(2,1)S(1)}, u32[]{:S(2)}, u32[]{:S(2)}) collective-permute-start(bf16[2,4,24,3072]{3,2,1,0:T(8,128)(2,1)S(1)} %dynamic-slice_bitcast_fusion.3), channel_id=1, source_target_pairs={{0,16},{1,17},{2,18},{3,19},{4,20},{5,21},{6,22},{7,23},{8,24},{9,... | collective-permute-start | bytes 3538952 | tf_op jit(solution)/shard_map/ppermute | solution.py:46
  442.3 28.2 %collective-permute-start.33 = (bf16[2,4,24,3072]{3,2,1,0:T(8,128)(2,1)S(1)}, bf16[2,4,24,3072]{3,2,1,0:T(8,128)(2,1)S(1)}, u32[]{:S(2)}, u32[]{:S(2)}) collective-permute-start(bf16[2,4,24,3072]{3,2,1,0:T(8,128)(2,1)S(1)} %dynamic-slice_bitcast_fusion.4), channel_id=1, source_target_pairs={{0,8},{1,9},{2,10},{3,11},{4,12},{5,13},{6,14},{7,15},{8,0},{9,1},... | collective-permute-start | bytes 3538952 | tf_op jit(solution)/shard_map/ppermute | solution.py:46
  444.1 39.2 %collective-permute-start.26 = (bf16[2,2,4,24,3328]{4,3,2,1,0:T(8,128)(2,1)S(1)}, bf16[2,2,4,24,3328]{4,3,2,1,0:T(8,128)(2,1)S(1)}, u32[]{:S(2)}, u32[]{:S(2)}) collective-permute-start(bf16[2,2,4,24,3328]{4,3,2,1,0:T(8,128)(2,1)S(1)} %dynamic-slice_bitcast_fusion), channel_id=1, source_target_pairs={{0,1},{1,0},{2,3},{3,2},{4,5},{5,4},{6,7},{7,6},{8,9},{9,8},{10,11... | collective-permute-start | bytes 7667720 | tf_op jit(solution)/shard_map/ppermute | solution.py:46
  484.1 28.6 %collective-permute-start.27 = (bf16[2,4,24,3328]{3,2,1,0:T(8,128)(2,1)S(1)}, bf16[2,4,24,3328]{3,2,1,0:T(8,128)(2,1)S(1)}, u32[]{:S(2)}, u32[]{:S(2)}) collective-permute-start(bf16[2,4,24,3328]{3,2,1,0:T(8,128)(2,1)S(1)} %dynamic-slice_bitcast_fusion.2), channel_id=1, source_target_pairs={{0,8},{1,9},{2,10},{3,11},{4,12},{5,13},{6,14},{7,15},{8,0},{9,1},... | collective-permute-start | bytes 3833864 | tf_op jit(solution)/shard_map/ppermute | solution.py:46
  485.6 27.4 %collective-permute-start.41 = (bf16[24,3072]{1,0:T(8,128)(2,1)S(1)}, bf16[24,3072]{1,0:T(8,128)(2,1)S(1)}, u32[]{:S(2)}, u32[]{:S(2)}) collective-permute-start(bf16[24,3072]{1,0:T(8,128)(2,1)S(1)} %get-tuple-element.155), channel_id=1, source_target_pairs={{0,2},{1,3},{2,4},{3,5},{4,6},{5,7},{6,0},{7,1},{8,10},{9,11},{10,... | collective-permute-start | bytes 442376 | tf_op jit(solution)/shard_map/ppermute | solution.py:46
  485.7 27.4 %collective-permute-start.42 = (bf16[24,3072]{1,0:T(8,128)(2,1)S(1)}, bf16[24,3072]{1,0:T(8,128)(2,1)S(1)}, u32[]{:S(2)}, u32[]{:S(2)}) collective-permute-start(bf16[24,3072]{1,0:T(8,128)(2,1)S(1)} %get-tuple-element.157), channel_id=1, source_target_pairs={{0,4},{1,5},{2,6},{3,7},{4,0},{5,1},{6,2},{7,3},{8,12},{9,13},{10,... | collective-permute-start | bytes 442376 | tf_op jit(solution)/shard_map/ppermute | solution.py:46
  485.8 28.9 %collective-permute-start.43 = (bf16[24,3072]{1,0:T(8,128)(2,1)S(1)}, bf16[24,3072]{1,0:T(8,128)(2,1)S(1)}, u32[]{:S(2)}, u32[]{:S(2)}) collective-permute-start(bf16[24,3072]{1,0:T(8,128)(2,1)S(1)} %get-tuple-element.156), channel_id=1, source_target_pairs={{0,6},{1,7},{2,0},{3,1},{4,2},{5,3},{6,4},{7,5},{8,14},{9,15},{10,... | collective-permute-start | bytes 442376 | tf_op jit(solution)/shard_map/ppermute | solution.py:46
  489.7 42.0 %collective-permute-start.35 = (bf16[24,3072]{1,0:T(8,128)(2,1)S(1)}, bf16[24,3072]{1,0:T(8,128)(2,1)S(1)}, u32[]{:S(2)}, u32[]{:S(2)}) collective-permute-start(bf16[24,3072]{1,0:T(8,128)(2,1)S(1)} %get-tuple-element.158), channel_id=1, source_target_pairs={{0,2},{1,3},{2,4},{3,5},{4,6},{5,7},{6,0},{7,1},{8,10},{9,11},{10,... | collective-permute-start | bytes 442376 | tf_op jit(solution)/shard_map/ppermute | solution.py:46
  (46 other events, 520.5 us)
Sparse Core Ops, SparseCore 0:
  11.1 92.1 all-gather.1
